TPU v7x, 512 devices: a whole 4x4x16 slice. The times are simulated.
512 devices in a mesh: band: 32 (over z_hi, y, x), pair: 16 (over z_lo, core).
Axes of the slice: x: 4, y: 4, z: 16 (z_hi: 2, z_lo: 8; z = z_hi * 8 + z_lo), core: 2. Of those that a mesh axis runs over, the one named last changes fastest.
Arguments:
- orbitals: bfloat16 [64, 32, 1024], P('band'), may hold values from -6 to 6
- kernel: float32 [32, 1024], replicated, may hold values from 0 to 1.2, as said below
- occupations: float32 [64], replicated, may hold values from 0.04 to 0.99
- plan: int32 [32], replicated, may hold values from 0 to 31, each once
Outputs:
- exchange: float32 [64, 32, 1024], P('band', 'pair')
- slot_energy: float32 [32], P('pair')
Inputs may be any that keep to these rules, and one draw needn't show every extreme that they name: `plan`: each owner distance 0 to 31 appears exactly once. kernel is unchanged when any one frequency index i is replaced by (32 - i) % 32, and is not negative.
All inputs are finite; a program needn't handle non-finite values.
Results may differ from a plain program's by a relative error of at most 0.0004.
Values may be sent and summed in bfloat16 or wider, within the bound.
No kernel may reach another device: no remote copies, remote signals or barrier semaphores. Data moves between devices by JAX's collectives and lax.ppermute only.
A program may use at most 64 MiB of HBM per device.

v0:
```python
import functools
import math

import jax
import jax.numpy as jnp
import ml_dtypes
import numpy as np
from jax import lax
from jax.experimental import pallas as pl
from jax.experimental.pallas import tpu as pltpu
from jax.sharding import Mesh
from jax.sharding import PartitionSpec as P

AXES = ("zh", "y", "x", "zl", "core")
BAND = ("zh", "y", "x")
PAIR = ("zl", "core")
SIZES = (2, 4, 4, 8, 2)

STEPS = (
    ((2, 2), (2, 1)),
    ((2, 3), (3, 2)),
    ((3, 3), (3, 1)),
    ((0, 0), (1, 0)),
    ((0, 1), (0, 3)),
    ((1, 3), (1, 1)),
    ((0, 2), (3, 0)),
    ((1, 2), (2, 0)),
)


def step_of(zh, zl, core):
    return STEPS[zl if zh == 0 else SIZES[3] - 1 - zl][core]


def place(coords):
    flat = 0
    for size, at in zip(SIZES, coords):
        flat = flat * size + at
    return flat


def routes(move):
    return [(place(c), place(move(*c))) for c in np.ndindex(*SIZES)]


def same_half(zh, y, x, zl, core):
    dy, dx = step_of(zh, zl, core)
    return zh, y ^ dy, x ^ dx, zl, core


def other_half(zh, y, x, zl, core):
    dy, dx = step_of(zh, zl, core)
    return 1 - zh, y ^ dy, x ^ dx, SIZES[3] - 1 - zl, core


def mirror(zh, y, x, zl, core):
    return 1 - zh, y, x, SIZES[3] - 1 - zl, core


def other_core(zh, y, x, zl, core):
    return zh, y, x, zl, 1 - core


def two_parts(matrix):
    high = matrix.astype(ml_dtypes.bfloat16)
    low = (matrix - high.astype(np.float64)).astype(ml_dtypes.bfloat16)
    return np.stack([high, low])


def hartley(points):
    at = np.arange(points)
    angle = (np.outer(at, at) % points) * (2.0 * math.pi / points)
    return (np.cos(angle) + np.sin(angle)) / math.sqrt(points)


def mode_order(points):
    at = np.arange(points)
    return np.concatenate([at[0::4], at[2::4], at[1::2]])


@functools.cache
def tables(points, own, groups, cores):
    base = hartley(points)
    quarter = base[:, : points // 4]
    quarters = np.kron(quarter[0::4].T, base)
    halves = np.kron(quarter[2::4].T, base)
    odd = np.kron(base[1::2, : points // 2].T, base)
    pairs = own * own
    along = np.kron(np.eye(pairs), base)
    planes = points // groups
    rows = []
    for core in range(cores):
        for zl in range(groups // cores):
            for a in range(own):
                for low in range(planes):
                    rows.append((a, (zl * cores + core) * planes + low))
    picks = []
    spread = np.zeros((pairs * points, own * points))
    for b in range(own):
        for a, plane in rows:
            spread[len(picks), b * points + plane] = 1.0
            picks.append((b * own + a) * points + plane)
    return dict(
        along=two_parts(along).reshape(2 * pairs * points, pairs * points),
        back=two_parts(along[picks]).reshape(2 * pairs * points, pairs * points),
        spread=spread.astype(ml_dtypes.bfloat16),
        quarters=two_parts(quarters),
        halves=two_parts(halves),
        odd=two_parts(odd),
    )


NAMES = ("along", "back", "spread", "quarters", "halves", "odd")


def split(value):
    high = value.astype(jnp.bfloat16)
    return high, (value - high.astype(jnp.float32)).astype(jnp.bfloat16)


def product(left, right, contract):
    return lax.dot_general(left, right, (contract, ((), ())), preferred_element_type=jnp.float32)


def on_rows(value, matrix, contract):
    rows = value.shape[0]
    high, low = split(value)
    both = product(jnp.concatenate([high, low], axis=0), matrix[0], ((1,), (contract,)))
    rest = product(high, matrix[1], ((1,), (contract,)))
    return both[:rows] + both[rows:] + rest


def on_planes(matrix, value):
    rows = matrix.shape[0] // 2
    high, low = split(value)
    both = product(matrix, high, ((1,), (0,)))
    rest = product(matrix[:rows], low, ((1,), (0,)))
    return both[:rows] + both[rows:] + rest


def in_mode_order(kernel, points):
    order = mode_order(points)
    width = 128
    each = width // points
    lane = lax.broadcasted_iota(jnp.int32, (points, width), 1)
    columns = []
    for column in range(points * points // width):
        taken = None
        for at in range(each):
            source = int(order[column * each + at])
            block = kernel[:, source // each * width : (source // each + 1) * width]
            shift = (at - source % each) * points % width
            if shift:
                block = pltpu.roll(block, shift, 1)
            taken = block if taken is None else jnp.where(lane >= at * points, block, taken)
        columns.append(taken)
    return jnp.concatenate(columns, axis=1)


def pair_terms(mine, partner, mine_weight, partner_weight, kernel, table):
    own, points, cells = mine.shape
    pairs = own * own
    block = cells // 4
    left = mine.astype(jnp.float32)
    right = partner.astype(jnp.float32)
    modal = in_mode_order(kernel, points)
    along, back, spread = table["along"], table["back"], table["spread"]
    parts = []
    for at in range(4):
        lanes = slice(at * block, (at + 1) * block)
        density = jnp.concatenate(
            [left[a, :, lanes] * right[b, :, lanes] for b in range(own) for a in range(own)], axis=0
        )
        parts.append(on_planes(along, density))
    even0, even1 = parts[0] + parts[2], parts[1] + parts[3]
    odd = jnp.concatenate([parts[0] - parts[2], parts[1] - parts[3]], axis=1)
    spectrum = jnp.concatenate(
        [
            on_rows(even0 + even1, table["quarters"], 0),
            on_rows(even0 - even1, table["halves"], 0),
            on_rows(odd, table["odd"], 0),
        ],
        axis=1,
    )
    energies = []
    shaped = []
    for f in range(pairs):
        rows = spectrum[f * points : (f + 1) * points]
        potential = rows * modal
        shaped.append(potential)
        terms = (rows * potential).reshape(points // 8, 8, cells // 128, 128)
        energies.append(jnp.sum(terms, axis=(0, 2)))
    energy = jnp.zeros((8, 128), jnp.float32)
    straight = jnp.zeros((8, 128), jnp.float32)
    crossed = jnp.zeros((8, 128), jnp.float32)
    for b in range(own):
        for a in range(own):
            term = energies[b * own + a] * (mine_weight[a] * partner_weight[b])
            if a == b:
                straight = straight + term
            else:
                crossed = crossed + term
    energy = straight + crossed
    shaped = jnp.concatenate(shaped, axis=0)
    quarters = on_rows(shaped[:, :block], table["quarters"], 1)
    halves = on_rows(shaped[:, block : 2 * block], table["halves"], 1)
    odd = on_rows(shaped[:, 2 * block :], table["odd"], 1)
    even0, even1 = quarters + halves, quarters - halves
    odd0, odd1 = odd[:, :block], odd[:, block:]
    fields = [even0 + odd0, even1 + odd1, even0 - odd0, even1 - odd1]
    flat = partner.reshape(own * points, cells)
    rows = own * points
    pulled = []
    for at in range(4):
        potential = on_planes(back, fields[at])
        spreads = product(spread, flat[:, at * block : (at + 1) * block], ((1,), (0,)))
        total = None
        for b in range(own):
            term = potential[b * rows : (b + 1) * rows] * spreads[b * rows : (b + 1) * rows]
            term = term * partner_weight[b]
            total = term if total is None else total + term
        pulled.append(-total)
    return jnp.concatenate(pulled, axis=1), energy


def weights_of(occupation_ref, owner, own):
    return [occupation_ref[owner * own + at] for at in range(own)]


def first_body(who_ref, occupation_ref, mine_ref, partner_ref, kernel_ref, *refs):
    table = {name: ref[...] for name, ref in zip(NAMES, refs)}
    exchange_ref, energy_ref = refs[len(NAMES) :]
    own = mine_ref.shape[0]
    exchange, energy = pair_terms(
        mine_ref[...],
        partner_ref[...],
        weights_of(occupation_ref, who_ref[0], own),
        weights_of(occupation_ref, who_ref[1], own),
        kernel_ref[...],
        table,
    )
    exchange_ref[...] = exchange
    energy_ref[...] = jnp.full(energy_ref.shape, jnp.sum(energy))


def second_body(who_ref, occupation_ref, mine_ref, partner_ref, kernel_ref, *refs):
    table = {name: ref[...] for name, ref in zip(NAMES, refs)}
    before_ref, near_ref, far_ref, keep_ref, send_ref, energy_ref = refs[len(NAMES) :]
    own = mine_ref.shape[0]
    exchange, energy = pair_terms(
        mine_ref[...],
        partner_ref[...],
        weights_of(occupation_ref, who_ref[0], own),
        weights_of(occupation_ref, who_ref[2], own),
        kernel_ref[...],
        table,
    )
    exchange = exchange + before_ref[...]
    half = exchange.shape[0] // 2
    low, high = exchange[:half], exchange[half:]
    first = who_ref[3] == 0
    keep_ref[...] = jnp.where(first, low, high)
    send_ref[...] = jnp.where(first, high, low)
    lane = lax.broadcasted_iota(jnp.int32, energy_ref.shape, 1)
    energy_ref[...] = jnp.where(lane == 0, near_ref[...] + far_ref[...], jnp.full(energy_ref.shape, 2.0 * jnp.sum(energy)))


def in_vmem(count):
    return [pl.BlockSpec(memory_space=pltpu.VMEM)] * count


def in_smem(count):
    return [pl.BlockSpec(memory_space=pltpu.SMEM)] * count


def on_device(orbitals, kernel, occupations, plan):
    own, points, cells = orbitals.shape
    total_orbitals = occupations.shape[0]
    groups = lax.axis_size(PAIR)
    cores = lax.axis_size("core")
    chips = lax.axis_size("zl")
    slots = plan.shape[0] // groups
    column = lax.axis_size(("y", "x"))
    zh, zl, core = lax.axis_index("zh"), lax.axis_index("zl"), lax.axis_index("core")
    here = lax.axis_index(("y", "x"))
    steps = np.array([[dy * SIZES[2] + dx for dy, dx in chip] for chip in STEPS], np.int32)
    chip = jnp.where(zh == 0, zl, chips - 1 - zl)
    near_step = jnp.asarray(steps)[chip]
    step = near_step[core]
    owner = zh * column + here
    who = jnp.stack([owner, zh * column + (here ^ step), (1 - zh) * column + (here ^ step), core]).astype(jnp.int32)

    far = lax.ppermute(orbitals, AXES, routes(other_half))
    near = lax.ppermute(orbitals, AXES, routes(same_half))

    table = tables(points, own, groups, cores)
    constants = [jnp.asarray(table[name]) for name in NAMES]
    rows = own * points
    flops = 2 * 3 * own * own * points * cells * (own * own * points + 384) * 2
    cost = pl.CostEstimate(flops=flops, bytes_accessed=4 << 20, transcendentals=0)
    exchange, energy = pl.pallas_call(
        first_body,
        out_shape=(
            jax.ShapeDtypeStruct((rows, cells), jnp.float32),
            jax.ShapeDtypeStruct((8, 128), jnp.float32),
        ),
        in_specs=in_smem(2) + in_vmem(3 + len(NAMES)),
        out_specs=tuple(in_vmem(2)),
        cost_estimate=cost,
        name="near_pairs",
    )(who, occupations, orbitals, near, kernel, *constants)
    across = lax.ppermute(energy, AXES, routes(mirror))
    keep, send, energy = pl.pallas_call(
        second_body,
        out_shape=(
            jax.ShapeDtypeStruct((rows // 2, cells), jnp.float32),
            jax.ShapeDtypeStruct((rows // 2, cells), jnp.float32),
            jax.ShapeDtypeStruct((8, 128), jnp.float32),
        ),
        in_specs=in_smem(2) + in_vmem(6 + len(NAMES)),
        out_specs=tuple(in_vmem(3)),
        cost_estimate=cost,
        name="far_pairs",
    )(who, occupations, orbitals, far, kernel, *constants, exchange, energy, across)

    everyone = lax.all_to_all(
        jnp.broadcast_to(energy[:1, :], (column * cores, 128)), ("y", "x", "core"), 0, 0, tiled=True
    )
    received = lax.ppermute(send, AXES, routes(other_core))

    total = everyone[:, :2].reshape(column, cores, 2)
    while total.shape[0] > 1:
        half = total.shape[0] // 2
        total = total[:half] + total[half:]
    total = total[0]
    lane = jnp.arange(128, dtype=jnp.int32)
    levels = jnp.zeros((128,), jnp.float32)
    for at in range(cores):
        levels = levels + jnp.where(lane == near_step[at], total[at, 0], 0.0)
        levels = levels + jnp.where(lane == column + near_step[at], total[at, 1], 0.0)
    each = rows // 2 // chips
    summed = (keep + received).reshape(chips, each, cells)
    extra = jnp.broadcast_to(levels, (chips, each, 128))
    pieces = lax.all_to_all(jnp.concatenate([summed, extra], axis=2), "zl", 0, 0, tiled=True)
    result = jnp.sum(pieces, axis=0)
    exchange = result[:, :cells].reshape(own, each // own, cells)
    group = lax.axis_index(PAIR)
    mine_slots = lax.dynamic_slice_in_dim(plan, group * slots, slots)
    picked = jnp.where(lane[None] == mine_slots[:, None], result[:1, cells:], 0.0)
    slot_energy = -jnp.sum(picked, axis=1) / (2.0 * total_orbitals * points**3)
    return exchange, slot_energy


def solution(mesh):
    split_mesh = Mesh(mesh.devices.reshape(SIZES), AXES)
    return jax.shard_map(
        on_device,
        mesh=split_mesh,
        in_specs=(P(BAND, None, None), P(), P(), P()),
        out_specs=(P(BAND, PAIR, None), P(PAIR)),
        check_vma=False,
    )
```

profile of v0, /device:TPU:32, one launch (start us, length us, event | category | flops | bytes accessed | tf_op | source)
XLA Modules:
  0.0 81.7 jit_solution(9115846002167885105)
XLA Ops:
  0.6 7.3 %collective-permute-start.1 = (bf16[2,32,1024]{2,1,0:T(8,128)(2,1)}, bf16[2,32,1024]{2,1,0:T(8,128)(2,1)S(1)}, u32[]{:S(2)}, u32[]{:S(2)}) collective-permute-start(bf16[2,32,1024]{2,1,0:T(8,128)(2,1)} %mine_ref.3), channel_id=1, source_target_pairs={{0,160},{1,145},{2,178},{3,227},{4,244},{5,213},{6,6},{7,71},{8,24... | collective-permute-start | bytes 393224 | tf_op jit(solution)/shard_map/ppermute | solution.py:294
  7.9 11.1 %collective-permute-start = (bf16[2,32,1024]{2,1,0:T(8,128)(2,1)}, bf16[2,32,1024]{2,1,0:T(8,128)(2,1)S(1)}, u32[]{:S(2)}, u32[]{:S(2)}) collective-permute-start(bf16[2,32,1024]{2,1,0:T(8,128)(2,1)} %mine_ref.3), channel_id=1, source_target_pairs={{0,430},{1,415},{2,444},{3,493},{4,506},{5,475},{6,264},{7,329},{8... | collective-permute-start | bytes 393224 | tf_op jit(solution)/shard_map/ppermute | solution.py:293
  19.1 1.3 %dynamic_slice.9 = s32[1,1]{1,0:T(1,128)} dynamic-slice(s32[8,2]{1,0:T(8,128)} %constant.68.clone, s32[]{:T(128)S(6)} %select_n.36, s32[]{:T(128)S(6)} %select_n.38), dynamic_slice_sizes={1,1} | dynamic-slice | bytes 12 | tf_op jit(solution)/shard_map/dynamic_slice | solution.py:289
  21.0 0.6 pad_add_fusion.who_ref
  21.6 0.6 copy-done.2
  22.2 4.1 %near_pairs.1 = (f32[64,1024]{1,0:T(8,128)}, f32[8,128]{1,0:T(8,128)}) custom-call(s32[4]{0:T(128)} %pad_add_fusion.who_ref, f32[64]{0:T(128)} %occupation_ref.3, bf16[2,32,1024]{2,1,0:T(8,128)(2,1)} %mine_ref.3, bf16[2,32,1024]{2,1,0:T(8,128)(2,1)} %copy-done.2, f32[32,1024]{1,0:T(8,128)} %kernel_ref.3, bf16[256,128]{1,0:T(8,128)(2,1)} %constant.69.clone.refs_0_, ...), custom_call_target="tpu_custom_call" | custom-call | flops 805306368 | bytes 4194304 | tf_op jit(solution)/shard_map/near_pairs/pallas_call | solution.py:301
  26.3 2.2 %collective-permute-start.2 = (f32[8,128]{1,0:T(8,128)}, f32[8,128]{1,0:T(8,128)S(1)}, u32[]{:S(2)}, u32[]{:S(2)}) collective-permute-start(f32[8,128]{1,0:T(8,128)} %get-tuple-element.8.refs_7_), channel_id=1, source_target_pairs={{0,270},{1,271},{2,268},{3,269},{4,266},{5,267},{6,264},{7,265},{8... | collective-permute-start | bytes 12296 | tf_op jit(solution)/shard_map/ppermute | solution.py:312
  28.5 0.7 constant_dynamic-slice_fusion
  29.2 5.8 %collective-permute-done.2.refs_8_ = f32[8,128]{1,0:T(8,128)S(1)} collective-permute-done((f32[8,128]{1,0:T(8,128)}, f32[8,128]{1,0:T(8,128)S(1)}, u32[]{:S(2)}, u32[]{:S(2)}) %collective-permute-start.2) | collective-permute-done | bytes 4128 | tf_op jit(solution)/shard_map/ppermute | solution.py:312
  35.0 0.6 copy-done.3
  35.6 4.1 %far_pairs.1 = (f32[32,1024]{1,0:T(8,128)}, f32[32,1024]{1,0:T(8,128)}, f32[8,128]{1,0:T(8,128)}) custom-call(s32[4]{0:T(128)} %pad_add_fusion.who_ref, f32[64]{0:T(128)} %occupation_ref.3, bf16[2,32,1024]{2,1,0:T(8,128)(2,1)} %mine_ref.3, bf16[2,32,1024]{2,1,0:T(8,128)(2,1)} %copy-done.1, f32[32,1024]{1,0:T(8,128)} %kernel_ref.3, ...), custom_call_target="tpu_custom_call" | custom-call | flops 805306368 | bytes 4194304 | tf_op jit(solution)/shard_map/far_pairs/pallas_call | solution.py:313
  39.8 0.7 slice_bitcast_fusion.1
  40.5 0.6 broadcast_in_dim.44
  41.1 7.1 %all-to-all-start = ((f32[32,1,128]{2,1,0:T(1,128)}), f32[32,1,128]{2,1,0:T(1,128)S(1)}, u32[]{:S(2)}, u32[]{:S(2)}) async-start(f32[32,1,128]{2,1,0:T(1,128)} %broadcast_in_dim.44), calls=%async_computation | async-start | bytes 32768 | tf_op jit(solution)/shard_map/all_to_all | solution.py:326
  48.2 0.6 fusion.5
  50.1 2.2 %collective-permute-start.3 = (f32[32,1024]{1,0:T(8,128)}, f32[32,1024]{1,0:T(8,128)S(1)}, u32[]{:S(2)}, u32[]{:S(2)}) collective-permute-start(f32[32,1024]{1,0:T(8,128)} %get-tuple-element.10), channel_id=1, source_target_pairs={{0,1},{1,0},{2,3},{3,2},{4,5},{5,4},{6,7},{7,6},{8,9},{9,8},{10,11... | collective-permute-start | bytes 393224 | tf_op jit(solution)/shard_map/ppermute | solution.py:329
  52.2 3.2 %all-to-all-done = f32[32,1,128]{2,1,0:T(1,128)S(1)} async-done(((f32[32,1,128]{2,1,0:T(1,128)}), f32[32,1,128]{2,1,0:T(1,128)S(1)}, u32[]{:S(2)}, u32[]{:S(2)}) %all-to-all-start) | async-done | bytes 16416 | tf_op jit(solution)/shard_map/all_to_all | solution.py:326
  55.5 0.7 fusion.4
  56.1 3.7 %fusion.3 = f32[128]{0:T(128)S(1)} fusion(f32[]{:T(128)} %bitcast.12, s32[]{:T(128)S(6)} %add.74, f32[]{:T(128)} %bitcast.11, s32[]{:T(128)} %bitcast.10, f32[]{:T(128)} %bitcast.9, s32[]{:T(128)S(6)} %add.71, f32[]{:T(128)} %bitcast.8, s32[]{:T(128)} %bitcast.5), kind=kLoop, calls=%fused_computation.13 | loop fusion | flops 1408 | bytes 544 | tf_op jit(solution)/shard_map/add | solution.py:340
  60.0 0.7 pad_maximum_fusion
  60.7 7.9 %all-to-all-start.1 = ((f32[8,4,1152]{2,1,0:T(4,128)}), f32[8,4,1152]{2,1,0:T(4,128)S(1)}, u32[]{:S(2)}, u32[]{:S(2)}) async-start(f32[8,4,1152]{2,1,0:T(4,128)} %pad_maximum_fusion), calls=%async_computation.1 | async-start | bytes 294912 | tf_op jit(solution)/shard_map/all_to_all | solution.py:344
  68.5 0.7 copy-done.4
  69.3 11.0 %all-to-all-done.1 = f32[8,4,1152]{2,1,0:T(4,128)S(1)} async-done(((f32[8,4,1152]{2,1,0:T(4,128)}), f32[8,4,1152]{2,1,0:T(4,128)S(1)}, u32[]{:S(2)}, u32[]{:S(2)}) %all-to-all-start.1) | async-done | bytes 147488 | tf_op jit(solution)/shard_map/all_to_all | solution.py:344
  80.3 0.6 reshape.38
  (23 shorter events, 0.9 us)
Async XLA Ops:
  0.6 20.9 %collective-permute-start.1 = (bf16[2,32,1024]{2,1,0:T(8,128)(2,1)}, bf16[2,32,1024]{2,1,0:T(8,128)(2,1)S(1)}, u32[]{:S(2)}, u32[]{:S(2)}) collective-permute-start(bf16[2,32,1024]{2,1,0:T(8,128)(2,1)} %mine_ref.3), channel_id=1, source_target_pairs={{0,160},{1,145},{2,178},{3,227},{4,244},{5,213},{6,6},{7,71},{8,24... | collective-permute-start | bytes 393224 | tf_op jit(solution)/shard_map/ppermute | solution.py:294
  7.9 21.3 %collective-permute-start = (bf16[2,32,1024]{2,1,0:T(8,128)(2,1)}, bf16[2,32,1024]{2,1,0:T(8,128)(2,1)S(1)}, u32[]{:S(2)}, u32[]{:S(2)}) collective-permute-start(bf16[2,32,1024]{2,1,0:T(8,128)(2,1)} %mine_ref.3), channel_id=1, source_target_pairs={{0,430},{1,415},{2,444},{3,493},{4,506},{5,475},{6,264},{7,329},{8... | collective-permute-start | bytes 393224 | tf_op jit(solution)/shard_map/ppermute | solution.py:293
  21.6 0.6 copy-start.2
  26.3 8.7 %collective-permute-start.2 = (f32[8,128]{1,0:T(8,128)}, f32[8,128]{1,0:T(8,128)S(1)}, u32[]{:S(2)}, u32[]{:S(2)}) collective-permute-start(f32[8,128]{1,0:T(8,128)} %get-tuple-element.8.refs_7_), channel_id=1, source_target_pairs={{0,270},{1,271},{2,268},{3,269},{4,266},{5,267},{6,264},{7,265},{8... | collective-permute-start | bytes 12296 | tf_op jit(solution)/shard_map/ppermute | solution.py:312
  29.2 5.8 %copy-start.1 = (bf16[2,32,1024]{2,1,0:T(8,128)(2,1)}, bf16[2,32,1024]{2,1,0:T(8,128)(2,1)S(1)}, u32[]{:S(2)}) copy-start(bf16[2,32,1024]{2,1,0:T(8,128)(2,1)S(1)} %collective-permute-done.partner_ref) | copy-start | bytes 393220
  35.0 0.6 copy-start.3
  39.7 20.1 %copy-start = (f32[32,1024]{1,0:T(8,128)S(1)}, f32[32,1024]{1,0:T(8,128)}, u32[]{:S(2)}) copy-start(f32[32,1024]{1,0:T(8,128)} %get-tuple-element.9) | copy-start | bytes 393220
  41.1 14.4 %all-to-all-start = ((f32[32,1,128]{2,1,0:T(1,128)}), f32[32,1,128]{2,1,0:T(1,128)S(1)}, u32[]{:S(2)}, u32[]{:S(2)}) async-start(f32[32,1,128]{2,1,0:T(1,128)} %broadcast_in_dim.44), calls=%async_computation | async-start | bytes 32768 | tf_op jit(solution)/shard_map/all_to_all | solution.py:326
  50.1 9.8 %collective-permute-start.3 = (f32[32,1024]{1,0:T(8,128)}, f32[32,1024]{1,0:T(8,128)S(1)}, u32[]{:S(2)}, u32[]{:S(2)}) collective-permute-start(f32[32,1024]{1,0:T(8,128)} %get-tuple-element.10), channel_id=1, source_target_pairs={{0,1},{1,0},{2,3},{3,2},{4,5},{5,4},{6,7},{7,6},{8,9},{9,8},{10,11... | collective-permute-start | bytes 393224 | tf_op jit(solution)/shard_map/ppermute | solution.py:329
  60.7 19.6 %all-to-all-start.1 = ((f32[8,4,1152]{2,1,0:T(4,128)}), f32[8,4,1152]{2,1,0:T(4,128)S(1)}, u32[]{:S(2)}, u32[]{:S(2)}) async-start(f32[8,4,1152]{2,1,0:T(4,128)} %pad_maximum_fusion), calls=%async_computation.1 | async-start | bytes 294912 | tf_op jit(solution)/shard_map/all_to_all | solution.py:344
  68.5 0.7 copy-start.4
where the time goes:
time: 82.2 us; the launch traced here: 81.7 us
  starting transfers between devices  37.7 us (46%)
  waiting for transfers between devices  20 us (24%)
  Pallas kernels  8.23 us (10%)
  local copies, waits for them, and re-layouts  7.25 us (9%)
  other arithmetic  5.76 us (7%)
  between operations  2.68 us (3%)
    ppermute x1, starting transfers between devices, on_device(): far = lax.ppermute(orbitals, AXES, routes(other_half))  11.1 us
    all_to_all x1, waiting for transfers between devices, on_device(): lax.all_to_all(jnp.concatenate([summed, extra], axis=2), 'zl', 0, 0, tile...  11 us
    all_to_all x1, starting transfers between devices, on_device(): lax.all_to_all(jnp.concatenate([summed, extra], axis=2), 'zl', 0, 0, tile...  7.88 us
    ppermute x1, starting transfers between devices, on_device(): near = lax.ppermute(orbitals, AXES, routes(same_half))  7.3 us
    all_to_all x1, starting transfers between devices, on_device(): lax.all_to_all(jnp.broadcast_to(energy[:1, :], (column * cores, 128)), ('...  7.06 us
    ppermute x1, waiting for transfers between devices, on_device(): across = lax.ppermute(energy, AXES, routes(mirror))  5.77 us
    pallas_call x1, Pallas kernels, on_device(): pl.pallas_call(second_body, out_shape=(jax.ShapeDtypeStruct((rows // 2, c...  4.14 us
    pallas_call x1, Pallas kernels, on_device(): pl.pallas_call(first_body, out_shape=(jax.ShapeDtypeStruct((rows, cells),...  4.09 us
  transfers between devices with their start and end apart: 6, of which 3 were waited for; matrix products, arithmetic and copies ran while one was open for 9% of the time, Pallas kernels for 5%

commit v1 on v0

--- a/solution.py
+++ b/solution.py
@@ -227,15 +227,26 @@
     return [occupation_ref[owner * own + at] for at in range(own)]
 
 
-def first_body(who_ref, occupation_ref, mine_ref, partner_ref, kernel_ref, *refs):
+def whereabouts(steps_ref):
+    zh, zl, core = lax.axis_index("zh"), lax.axis_index("zl"), lax.axis_index("core")
+    here = lax.axis_index("y") * SIZES[2] + lax.axis_index("x")
+    column = SIZES[1] * SIZES[2]
+    chip = jnp.where(zh == 0, zl, SIZES[3] - 1 - zl)
+    step = steps_ref[chip * SIZES[4] + core]
+    there = jnp.bitwise_xor(here, step)
+    return core, step, zh * column + here, zh * column + there, (1 - zh) * column + there
+
+
+def first_body(steps_ref, occupation_ref, mine_ref, partner_ref, kernel_ref, *refs):
     table = {name: ref[...] for name, ref in zip(NAMES, refs)}
     exchange_ref, energy_ref = refs[len(NAMES) :]
     own = mine_ref.shape[0]
+    _, _, owner, near, _ = whereabouts(steps_ref)
     exchange, energy = pair_terms(
         mine_ref[...],
         partner_ref[...],
-        weights_of(occupation_ref, who_ref[0], own),
-        weights_of(occupation_ref, who_ref[1], own),
+        weights_of(occupation_ref, owner, own),
+        weights_of(occupation_ref, near, own),
         kernel_ref[...],
         table,
     )
@@ -243,26 +254,59 @@
     energy_ref[...] = jnp.full(energy_ref.shape, jnp.sum(energy))
 
 
-def second_body(who_ref, occupation_ref, mine_ref, partner_ref, kernel_ref, *refs):
+def second_body(steps_ref, occupation_ref, mine_ref, partner_ref, kernel_ref, *refs):
     table = {name: ref[...] for name, ref in zip(NAMES, refs)}
-    before_ref, near_ref, far_ref, keep_ref, send_ref, energy_ref = refs[len(NAMES) :]
+    before_ref, near_ref, across_ref, keep_ref, send_ref, energy_ref = refs[len(NAMES) :]
     own = mine_ref.shape[0]
+    core, step, owner, _, far = whereabouts(steps_ref)
     exchange, energy = pair_terms(
         mine_ref[...],
         partner_ref[...],
-        weights_of(occupation_ref, who_ref[0], own),
-        weights_of(occupation_ref, who_ref[2], own),
+        weights_of(occupation_ref, owner, own),
+        weights_of(occupation_ref, far, own),
         kernel_ref[...],
         table,
     )
     exchange = exchange + before_ref[...]
     half = exchange.shape[0] // 2
     low, high = exchange[:half], exchange[half:]
-    first = who_ref[3] == 0
-    keep_ref[...] = jnp.where(first, low, high)
-    send_ref[...] = jnp.where(first, high, low)
-    lane = lax.broadcasted_iota(jnp.int32, energy_ref.shape, 1)
-    energy_ref[...] = jnp.where(lane == 0, near_ref[...] + far_ref[...], jnp.full(energy_ref.shape, 2.0 * jnp.sum(energy)))
+    keep_ref[...] = jnp.where(core == 0, low, high)
+    send_ref[...] = jnp.where(core == 0, high, low)
+    lane = lax.broadcasted_iota(jnp.int32, near_ref.shape, 1)
+    near_total = near_ref[...] + across_ref[...]
+    far_total = jnp.full(near_ref.shape, 2.0 * jnp.sum(energy))
+    row = jnp.where(lane == step, near_total, jnp.where(lane == SIZES[1] * SIZES[2] + step, far_total, 0.0))
+    energy_ref[...] = jnp.broadcast_to(row[None], energy_ref.shape)
+
+
+def join_body(keep_ref, received_ref, energies_ref, out_ref):
+    chips, each, width = out_ref.shape
+    cells = keep_ref.shape[1]
+    rows = energies_ref[:, 0, :]
+    while rows.shape[0] > 8:
+        half = rows.shape[0] // 2
+        rows = rows[:half] + rows[half:]
+    for shift in (4, 2, 1):
+        rows = rows + pltpu.roll(rows, shift, 0)
+    out_ref[:, :, :cells] = (keep_ref[...] + received_ref[...]).reshape(chips, each, cells)
+    out_ref[:, :, cells:] = jnp.broadcast_to(rows[None, :each], (chips, each, width - cells))
+
+
+def last_body(scale, plan_ref, pieces_ref, exchange_ref, slot_ref):
+    chips, each, width = pieces_ref.shape
+    own, planes, cells = exchange_ref.shape
+    total = pieces_ref[0]
+    for chip in range(1, chips):
+        total = total + pieces_ref[chip]
+    for a in range(own):
+        exchange_ref[a] = total[a * planes : (a + 1) * planes, :cells]
+    levels = total[:1, cells:]
+    lane = lax.broadcasted_iota(jnp.int32, levels.shape, 1)
+    slots = slot_ref.shape[0]
+    group = lax.axis_index("zl") * SIZES[4] + lax.axis_index("core")
+    for slot in range(slots):
+        level = plan_ref[group * slots + slot]
+        slot_ref[slot] = jnp.sum(jnp.where(lane == level, levels, 0.0)) * scale
 
 
 def in_vmem(count):
@@ -271,6 +315,13 @@
 
 def in_smem(count):
     return [pl.BlockSpec(memory_space=pltpu.SMEM)] * count
+
+
+def floats(*shape):
+    return jax.ShapeDtypeStruct(shape, jnp.float32)
+
+
+PARAMS = pltpu.CompilerParams(vmem_limit_bytes=24 << 20)
 
 
 def on_device(orbitals, kernel, occupations, plan):
@@ -281,74 +332,56 @@
     chips = lax.axis_size("zl")
     slots = plan.shape[0] // groups
     column = lax.axis_size(("y", "x"))
-    zh, zl, core = lax.axis_index("zh"), lax.axis_index("zl"), lax.axis_index("core")
-    here = lax.axis_index(("y", "x"))
-    steps = np.array([[dy * SIZES[2] + dx for dy, dx in chip] for chip in STEPS], np.int32)
-    chip = jnp.where(zh == 0, zl, chips - 1 - zl)
-    near_step = jnp.asarray(steps)[chip]
-    step = near_step[core]
-    owner = zh * column + here
-    who = jnp.stack([owner, zh * column + (here ^ step), (1 - zh) * column + (here ^ step), core]).astype(jnp.int32)
-
+
+    near = lax.ppermute(orbitals, AXES, routes(same_half))
     far = lax.ppermute(orbitals, AXES, routes(other_half))
-    near = lax.ppermute(orbitals, AXES, routes(same_half))
 
     table = tables(points, own, groups, cores)
+    steps = jnp.asarray(np.array([dy * SIZES[2] + dx for chip in STEPS for dy, dx in chip], np.int32))
     constants = [jnp.asarray(table[name]) for name in NAMES]
     rows = own * points
+    each = rows // 2 // chips
     flops = 2 * 3 * own * own * points * cells * (own * own * points + 384) * 2
     cost = pl.CostEstimate(flops=flops, bytes_accessed=4 << 20, transcendentals=0)
     exchange, energy = pl.pallas_call(
         first_body,
-        out_shape=(
-            jax.ShapeDtypeStruct((rows, cells), jnp.float32),
-            jax.ShapeDtypeStruct((8, 128), jnp.float32),
-        ),
+        out_shape=(floats(rows, cells), floats(1, 128)),
         in_specs=in_smem(2) + in_vmem(3 + len(NAMES)),
         out_specs=tuple(in_vmem(2)),
         cost_estimate=cost,
+        compiler_params=PARAMS,
         name="near_pairs",
-    )(who, occupations, orbitals, near, kernel, *constants)
+    )(steps, occupations, orbitals, near, kernel, *constants)
     across = lax.ppermute(energy, AXES, routes(mirror))
-    keep, send, energy = pl.pallas_call(
+    keep, send, energies = pl.pallas_call(
         second_body,
-        out_shape=(
-            jax.ShapeDtypeStruct((rows // 2, cells), jnp.float32),
-            jax.ShapeDtypeStruct((rows // 2, cells), jnp.float32),
-            jax.ShapeDtypeStruct((8, 128), jnp.float32),
-        ),
+        out_shape=(floats(rows // 2, cells), floats(rows // 2, cells), floats(column * cores, 1, 128)),
         in_specs=in_smem(2) + in_vmem(6 + len(NAMES)),
         out_specs=tuple(in_vmem(3)),
         cost_estimate=cost,
+        compiler_params=PARAMS,
         name="far_pairs",
-    )(who, occupations, orbitals, far, kernel, *constants, exchange, energy, across)
-
-    everyone = lax.all_to_all(
-        jnp.broadcast_to(energy[:1, :], (column * cores, 128)), ("y", "x", "core"), 0, 0, tiled=True
-    )
+    )(steps, occupations, orbitals, far, kernel, *constants, exchange, energy, across)
+
+    everyone = lax.all_to_all(energies, ("y", "x", "core"), 0, 0, tiled=True)
     received = lax.ppermute(send, AXES, routes(other_core))
-
-    total = everyone[:, :2].reshape(column, cores, 2)
-    while total.shape[0] > 1:
-        half = total.shape[0] // 2
-        total = total[:half] + total[half:]
-    total = total[0]
-    lane = jnp.arange(128, dtype=jnp.int32)
-    levels = jnp.zeros((128,), jnp.float32)
-    for at in range(cores):
-        levels = levels + jnp.where(lane == near_step[at], total[at, 0], 0.0)
-        levels = levels + jnp.where(lane == column + near_step[at], total[at, 1], 0.0)
-    each = rows // 2 // chips
-    summed = (keep + received).reshape(chips, each, cells)
-    extra = jnp.broadcast_to(levels, (chips, each, 128))
-    pieces = lax.all_to_all(jnp.concatenate([summed, extra], axis=2), "zl", 0, 0, tiled=True)
-    result = jnp.sum(pieces, axis=0)
-    exchange = result[:, :cells].reshape(own, each // own, cells)
-    group = lax.axis_index(PAIR)
-    mine_slots = lax.dynamic_slice_in_dim(plan, group * slots, slots)
-    picked = jnp.where(lane[None] == mine_slots[:, None], result[:1, cells:], 0.0)
-    slot_energy = -jnp.sum(picked, axis=1) / (2.0 * total_orbitals * points**3)
-    return exchange, slot_energy
+    joined = pl.pallas_call(
+        join_body,
+        out_shape=floats(chips, each, cells + 128),
+        in_specs=in_vmem(3),
+        out_specs=in_vmem(1)[0],
+        compiler_params=PARAMS,
+        name="join",
+    )(keep, received, everyone)
+    pieces = lax.all_to_all(joined, "zl", 0, 0, tiled=True)
+    return pl.pallas_call(
+        functools.partial(last_body, -1.0 / (2.0 * total_orbitals * points**3)),
+        out_shape=(floats(own, each // own, cells), floats(slots)),
+        in_specs=in_smem(1) + in_vmem(1),
+        out_specs=(in_vmem(1)[0], in_smem(1)[0]),
+        compiler_params=PARAMS,
+        name="last",
+    )(plan, pieces)
 
 
 def solution(mesh):

time: 82.2 us -> 78.4 us (0.954)
  blocking collectives: 0 us -> 33.8 us
  waiting for transfers between devices: 20 us -> 4.1 us
  starting transfers between devices: 37.7 us -> 24.7 us
  other arithmetic: 5.76 us -> 0 us
  Pallas kernels: 8.23 us -> 5.86 us
  between operations: 2.68 us -> 0.73 us
  local copies, waits for them, and re-layouts: 7.25 us -> 8.69 us
    all_to_all x0 -> x2, blocking collectives: none -> 33.8 us  [the longest x1 19.5 us: on_device(): pieces = lax.all_to_all(joined, 'zl', 0, 0, tiled=True)]
    all_to_all x2 -> x0, starting transfers between devices: 14.9 us -> none  [the longest x1 7.88 us: on_device(): lax.all_to_all(jnp.concatenate([summed, extra], axis=2), 'zl', 0, 0, tile...]
    all_to_all x2 -> x0, waiting for transfers between devices: 14.2 us -> none  [the longest x1 11 us: on_device(): lax.all_to_all(jnp.concatenate([summed, extra], axis=2), 'zl', 0, 0, tile...]
    unnamed x10 -> x28, local copies, waits for them, and re-layouts: 1.89 us -> 8.69 us
    add x6 -> x0, other arithmetic: 3.76 us -> none  [the longest x1 3.71 us: on_device(): levels + jnp.where(lane == column + near_step[at], total[at, 1], 0.0)]
    pallas_call x2 -> x4, Pallas kernels: 8.23 us -> 5.86 us  [the longest x1 2.32 us: on_device(): pl.pallas_call(first_body, out_shape=(floats(rows, cells), floats(1, 128)...]
    ppermute x1, starting transfers between devices: 2.22 us -> 4.36 us  [on_device(): across = lax.ppermute(energy, AXES, routes(mirror))]
    dynamic_slice x3 -> x0, local copies, waits for them, and re-layouts: 2.05 us -> none  [the longest x1 1.28 us: on_device(): step = near_step[core]]
  transfers between devices with their start and end apart: 6 -> 4, of which waited for: 3 -> 1; matrix products, arithmetic and copies ran while one was open for 9% -> 0% of each run, Pallas kernels for 5% -> 3%
where the time goes in v1:
time: 78.4 us; the launch traced here: 77.8 us
  blocking collectives  33.8 us (43%)
  starting transfers between devices  24.7 us (32%)
  local copies, waits for them, and re-layouts  8.69 us (11%)
  Pallas kernels  5.86 us (7%)
  waiting for transfers between devices  4.1 us (5%)
    all_to_all x1, blocking collectives, on_device(): pieces = lax.all_to_all(joined, 'zl', 0, 0, tiled=True)  19.5 us
    all_to_all x1, blocking collectives, on_device(): everyone = lax.all_to_all(energies, ('y', 'x', 'core'), 0, 0, tiled=True)  14.3 us
    ppermute x1, starting transfers between devices, on_device(): far = lax.ppermute(orbitals, AXES, routes(other_half))  11.1 us
    unnamed x28, local copies, waits for them, and re-layouts  8.69 us
    ppermute x1, starting transfers between devices, on_device(): near = lax.ppermute(orbitals, AXES, routes(same_half))  7.3 us
    ppermute x1, starting transfers between devices, on_device(): across = lax.ppermute(energy, AXES, routes(mirror))  4.36 us
    ppermute x1, waiting for transfers between devices, on_device(): across = lax.ppermute(energy, AXES, routes(mirror))  4.09 us
    pallas_call x1, Pallas kernels, on_device(): pl.pallas_call(first_body, out_shape=(floats(rows, cells), floats(1, 128)...  2.32 us
  transfers between devices with their start and end apart: 4, of which 1 were waited for; matrix products, arithmetic and copies ran while one was open for 0% of the time, Pallas kernels for 3%

profile of v1, /device:TPU:32, one launch (start us, length us, event | category | flops | bytes accessed | tf_op | source)
XLA Modules:
  0.0 77.8 jit_solution(11546728007034553986)
XLA Ops:
  0.6 7.3 %collective-permute-start.1 = (bf16[2,32,1024]{2,1,0:T(8,128)(2,1)}, bf16[2,32,1024]{2,1,0:T(8,128)(2,1)S(1)}, u32[]{:S(2)}, u32[]{:S(2)}) collective-permute-start(bf16[2,32,1024]{2,1,0:T(8,128)(2,1)} %mine_ref.3), channel_id=1, source_target_pairs={{0,160},{1,145},{2,178},{3,227},{4,244},{5,213},{6,6},{7,71},{8,24... | collective-permute-start | bytes 393224 | tf_op jit(solution)/shard_map/ppermute | solution.py:336
  7.9 11.1 %collective-permute-start = (bf16[2,32,1024]{2,1,0:T(8,128)(2,1)}, bf16[2,32,1024]{2,1,0:T(8,128)(2,1)S(1)}, u32[]{:S(2)}, u32[]{:S(2)}) collective-permute-start(bf16[2,32,1024]{2,1,0:T(8,128)(2,1)} %mine_ref.3), channel_id=1, source_target_pairs={{0,430},{1,415},{2,444},{3,493},{4,506},{5,475},{6,264},{7,329},{8... | collective-permute-start | bytes 393224 | tf_op jit(solution)/shard_map/ppermute | solution.py:337
  19.0 0.0 collective-permute-done.1.partner_ref
  19.0 0.9 %copy-done.1 = bf16[2,32,1024]{2,1,0:T(8,128)(2,1)S(1)} copy-done((bf16[2,32,1024]{2,1,0:T(8,128)(2,1)S(1)}, bf16[2,32,1024]{2,1,0:T(8,128)(2,1)}, u32[]{:S(2)}) %copy-start.1) | copy-done | bytes 131096
  19.9 0.9 %copy-done.2 = f32[32,1024]{1,0:T(8,128)S(1)} copy-done((f32[32,1024]{1,0:T(8,128)S(1)}, f32[32,1024]{1,0:T(8,128)}, u32[]{:S(2)}) %copy-start.2) | copy-done | bytes 131096
  20.8 0.7 copy-done.4
  21.5 1.2 %copy-done.5 = bf16[2,512,512]{2,1,0:T(8,128)(2,1)S(1)} copy-done((bf16[2,512,512]{2,1,0:T(8,128)(2,1)S(1)}, bf16[2,512,512]{2,1,0:T(8,128)(2,1)}, u32[]{:S(2)}) %copy-start.5) | copy-done | bytes 1048600
  22.7 0.9 %copy-done.7 = bf16[2,256,256]{2,1,0:T(8,128)(2,1)S(1)} copy-done((bf16[2,256,256]{2,1,0:T(8,128)(2,1)S(1)}, bf16[2,256,256]{2,1,0:T(8,128)(2,1)}, u32[]{:S(2)}) %copy-start.7) | copy-done | bytes 262168
  23.7 0.9 %copy-done.8 = bf16[2,256,256]{2,1,0:T(8,128)(2,1)S(1)} copy-done((bf16[2,256,256]{2,1,0:T(8,128)(2,1)S(1)}, bf16[2,256,256]{2,1,0:T(8,128)(2,1)}, u32[]{:S(2)}) %copy-start.8) | copy-done | bytes 262168
  24.6 0.8 %copy-done.9 = bf16[256,128]{1,0:T(8,128)(2,1)S(1)} copy-done((bf16[256,128]{1,0:T(8,128)(2,1)S(1)}, bf16[256,128]{1,0:T(8,128)(2,1)}, u32[]{:S(2)}) %copy-start.9) | copy-done | bytes 65560
  25.5 0.8 %copy-done.10 = bf16[256,128]{1,0:T(8,128)(2,1)S(1)} copy-done((bf16[256,128]{1,0:T(8,128)(2,1)S(1)}, bf16[256,128]{1,0:T(8,128)(2,1)}, u32[]{:S(2)}) %copy-start.10) | copy-done | bytes 65560
  26.3 0.8 copy-done.12
  27.1 0.7 copy-done.13
  27.7 2.3 %near_pairs.1 = (f32[64,1024]{1,0:T(8,128)S(1)}, f32[1,128]{1,0:T(1,128)S(1)}) custom-call(s32[16]{0:T(128)S(1)} %copy-done.13, f32[64]{0:T(128)S(1)} %copy-done.4, bf16[2,32,1024]{2,1,0:T(8,128)(2,1)S(1)} %copy-done.1, bf16[2,32,1024]{2,1,0:T(8,128)(2,1)S(1)} %collective-permute-done.1.partner_ref, f32[32,1024]{1,0:T(8,128)S(1)} %copy-done.2, ...), custom_call_target="tpu_custom_call" | custom-call | flops 805306368 | bytes 4194304 | tf_op jit(solution)/shard_map/near_pairs/pallas_call | solution.py:346
  30.1 4.4 %collective-permute-start.2 = (f32[1,128]{1,0:T(1,128)S(1)}, f32[1,128]{1,0:T(1,128)S(1)}, u32[]{:S(2)}, u32[]{:S(2)}) collective-permute-start(f32[1,128]{1,0:T(1,128)S(1)} %get-tuple-element.8.refs_7_), channel_id=1, source_target_pairs={{0,270},{1,271},{2,268},{3,269},{4,266},{5,267},{6,264},{7,265},{8... | collective-permute-start | bytes 1544 | tf_op jit(solution)/shard_map/ppermute | solution.py:355
  34.4 0.0 collective-permute-done.partner_ref
  34.4 4.1 %collective-permute-done.2.refs_8_ = f32[1,128]{1,0:T(1,128)S(1)} collective-permute-done((f32[1,128]{1,0:T(1,128)S(1)}, f32[1,128]{1,0:T(1,128)S(1)}, u32[]{:S(2)}, u32[]{:S(2)}) %collective-permute-start.2) | collective-permute-done | bytes 544 | tf_op jit(solution)/shard_map/ppermute | solution.py:355
  38.5 2.3 %far_pairs.1 = (f32[32,1024]{1,0:T(8,128)S(1)}, f32[32,1024]{1,0:T(8,128)S(1)}, f32[32,1,128]{2,1,0:T(1,128)S(1)}) custom-call(s32[16]{0:T(128)S(1)} %copy-done.13, f32[64]{0:T(128)S(1)} %copy-done.4, bf16[2,32,1024]{2,1,0:T(8,128)(2,1)S(1)} %copy-done.1, bf16[2,32,1024]{2,1,0:T(8,128)(2,1)S(1)} %collective-permute-done.partner_ref, ...), custom_call_target="tpu_custom_call" | custom-call | flops 805306368 | bytes 4194304 | tf_op jit(solution)/shard_map/far_pairs/pallas_call | solution.py:356
  40.9 1.9 %collective-permute-start.3 = (f32[32,1024]{1,0:T(8,128)S(1)}, f32[32,1024]{1,0:T(8,128)S(1)}, u32[]{:S(2)}, u32[]{:S(2)}) collective-permute-start(f32[32,1024]{1,0:T(8,128)S(1)} %get-tuple-element.10), channel_id=1, source_target_pairs={{0,1},{1,0},{2,3},{3,2},{4,5},{5,4},{6,7},{7,6},{8,9},{9,8},{10,11... | collective-permute-start | bytes 393224 | tf_op jit(solution)/shard_map/ppermute | solution.py:367
  42.8 14.3 %all_to_all.10.energies_ref = f32[32,1,128]{2,1,0:T(1,128)S(1)} all-to-all(f32[32,1,128]{2,1,0:T(1,128)S(1)} %get-tuple-element.11), channel_id=1, replica_groups=mesh['zh'=2,'y'=4,'x'=4,'zl'=8,'core'=2] {'y','x','core'}, dimensions={0} | all-to-all | bytes 32768 | tf_op jit(solution)/shard_map/all_to_all | solution.py:366
  57.1 0.0 collective-permute-done.3.received_ref
  57.2 0.0 copy-start
  57.2 19.5 %all_to_all.11.pieces_ref = f32[8,4,1152]{2,1,0:T(4,128)S(1)} all-to-all(f32[8,4,1152]{2,1,0:T(4,128)S(1)} %join.1), channel_id=1, replica_groups=mesh['zh'=2,'y'=4,'x'=4,'zl'=8,'core'=2] {'zl'}, dimensions={0} | all-to-all | bytes 294912 | tf_op jit(solution)/shard_map/all_to_all | solution.py:376
  76.6 1.2 %last.1 = (f32[2,2,1024]{2,1,0:T(2,128)}, f32[2]{0:T(128)}) custom-call(s32[32]{0:T(128)S(1)} %copy-done, f32[8,4,1152]{2,1,0:T(4,128)S(1)} %all_to_all.11.pieces_ref), custom_call_target="tpu_custom_call" | custom-call | tf_op jit(solution)/shard_map/last/pallas_call | solution.py:377
  (18 shorter events, 0.1 us)
Async XLA Ops:
  0.6 18.4 %collective-permute-start.1 = (bf16[2,32,1024]{2,1,0:T(8,128)(2,1)}, bf16[2,32,1024]{2,1,0:T(8,128)(2,1)S(1)}, u32[]{:S(2)}, u32[]{:S(2)}) collective-permute-start(bf16[2,32,1024]{2,1,0:T(8,128)(2,1)} %mine_ref.3), channel_id=1, source_target_pairs={{0,160},{1,145},{2,178},{3,227},{4,244},{5,213},{6,6},{7,71},{8,24... | collective-permute-start | bytes 393224 | tf_op jit(solution)/shard_map/ppermute | solution.py:336
  7.9 26.5 %collective-permute-start = (bf16[2,32,1024]{2,1,0:T(8,128)(2,1)}, bf16[2,32,1024]{2,1,0:T(8,128)(2,1)S(1)}, u32[]{:S(2)}, u32[]{:S(2)}) collective-permute-start(bf16[2,32,1024]{2,1,0:T(8,128)(2,1)} %mine_ref.3), channel_id=1, source_target_pairs={{0,430},{1,415},{2,444},{3,493},{4,506},{5,475},{6,264},{7,329},{8... | collective-permute-start | bytes 393224 | tf_op jit(solution)/shard_map/ppermute | solution.py:337
  19.0 0.9 %copy-start.1 = (bf16[2,32,1024]{2,1,0:T(8,128)(2,1)S(1)}, bf16[2,32,1024]{2,1,0:T(8,128)(2,1)}, u32[]{:S(2)}) copy-start(bf16[2,32,1024]{2,1,0:T(8,128)(2,1)} %mine_ref.3) | copy-start | bytes 393220
  19.9 0.9 %copy-start.2 = (f32[32,1024]{1,0:T(8,128)S(1)}, f32[32,1024]{1,0:T(8,128)}, u32[]{:S(2)}) copy-start(f32[32,1024]{1,0:T(8,128)} %kernel_ref.3) | copy-start | bytes 393220
  20.8 0.7 copy-start.4
  21.5 1.2 %copy-start.5 = (bf16[2,512,512]{2,1,0:T(8,128)(2,1)S(1)}, bf16[2,512,512]{2,1,0:T(8,128)(2,1)}, u32[]{:S(2)}) copy-start(bf16[2,512,512]{2,1,0:T(8,128)(2,1)} %constant.20.clone.refs_5_) | copy-start | bytes 3145732
  22.7 0.9 %copy-start.7 = (bf16[2,256,256]{2,1,0:T(8,128)(2,1)S(1)}, bf16[2,256,256]{2,1,0:T(8,128)(2,1)}, u32[]{:S(2)}) copy-start(bf16[2,256,256]{2,1,0:T(8,128)(2,1)} %constant.19.clone.refs_4_) | copy-start | bytes 786436
  23.7 0.9 %copy-start.8 = (bf16[2,256,256]{2,1,0:T(8,128)(2,1)S(1)}, bf16[2,256,256]{2,1,0:T(8,128)(2,1)}, u32[]{:S(2)}) copy-start(bf16[2,256,256]{2,1,0:T(8,128)(2,1)} %constant.18.clone.refs_3_) | copy-start | bytes 786436
  24.6 0.8 %copy-start.9 = (bf16[256,128]{1,0:T(8,128)(2,1)S(1)}, bf16[256,128]{1,0:T(8,128)(2,1)}, u32[]{:S(2)}) copy-start(bf16[256,128]{1,0:T(8,128)(2,1)} %constant.16.clone.refs_1_) | copy-start | bytes 196612
  25.5 0.8 %copy-start.10 = (bf16[256,128]{1,0:T(8,128)(2,1)S(1)}, bf16[256,128]{1,0:T(8,128)(2,1)}, u32[]{:S(2)}) copy-start(bf16[256,128]{1,0:T(8,128)(2,1)} %constant.15.clone.refs_0_) | copy-start | bytes 196612
  26.3 0.8 copy-start.12
  27.1 0.7 copy-start.13
  27.7 10.8 %copy-start.3 = (f32[32,1024]{1,0:T(8,128)S(1)}, f32[32,1024]{1,0:T(8,128)}, u32[]{:S(2)}) copy-start(f32[32,1024]{1,0:T(8,128)} %kernel_ref.3) | copy-start | bytes 393220
  27.7 10.8 %copy-start.6 = (bf16[2,512,512]{2,1,0:T(8,128)(2,1)S(1)}, bf16[2,512,512]{2,1,0:T(8,128)(2,1)}, u32[]{:S(2)}) copy-start(bf16[2,512,512]{2,1,0:T(8,128)(2,1)} %constant.20.clone.refs_5_) | copy-start | bytes 3145732
  27.7 10.8 %copy-start.11 = (bf16[256,128]{1,0:T(8,128)(2,1)S(1)}, bf16[256,128]{1,0:T(8,128)(2,1)}, u32[]{:S(2)}) copy-start(bf16[256,128]{1,0:T(8,128)(2,1)} %constant.15.clone.refs_0_) | copy-start | bytes 196612
  30.1 8.5 %collective-permute-start.2 = (f32[1,128]{1,0:T(1,128)S(1)}, f32[1,128]{1,0:T(1,128)S(1)}, u32[]{:S(2)}, u32[]{:S(2)}) collective-permute-start(f32[1,128]{1,0:T(1,128)S(1)} %get-tuple-element.8.refs_7_), channel_id=1, source_target_pairs={{0,270},{1,271},{2,268},{3,269},{4,266},{5,267},{6,264},{7,265},{8... | collective-permute-start | bytes 1544 | tf_op jit(solution)/shard_map/ppermute | solution.py:355
  40.9 16.3 %collective-permute-start.3 = (f32[32,1024]{1,0:T(8,128)S(1)}, f32[32,1024]{1,0:T(8,128)S(1)}, u32[]{:S(2)}, u32[]{:S(2)}) collective-permute-start(f32[32,1024]{1,0:T(8,128)S(1)} %get-tuple-element.10), channel_id=1, source_target_pairs={{0,1},{1,0},{2,3},{3,2},{4,5},{5,4},{6,7},{7,6},{8,9},{9,8},{10,11... | collective-permute-start | bytes 393224 | tf_op jit(solution)/shard_map/ppermute | solution.py:367
  57.2 19.5 %copy-start = (s32[32]{0:T(128)S(1)}, s32[32]{0:T(128)}, u32[]{:S(2)}) copy-start(s32[32]{0:T(128)} %plan_ref.1) | copy-start | bytes 388

commit v2 on v1

--- a/solution.py
+++ b/solution.py
@@ -100,17 +100,29 @@
         for a, plane in rows:
             spread[len(picks), b * points + plane] = 1.0
             picks.append((b * own + a) * points + plane)
+    square = lambda matrix: np.concatenate([two_parts(matrix)[part, :, at : at + 256] for part in range(2) for at in range(0, matrix.shape[1], 256)])
+    sides = np.concatenate([two_parts(along).reshape(-1, pairs * points), two_parts(along[picks]).reshape(-1, pairs * points)], axis=1)
+    blocks = [
+        square(quarters),
+        square(halves),
+        square(odd),
+        sides,
+        np.pad(spread, ((0, 0), (0, 256 - spread.shape[1]))).astype(ml_dtypes.bfloat16),
+    ]
+    return np.concatenate(blocks)
+
+
+def unpacked(ref, own, points):
+    side = own * own * points
+    big = [jnp.concatenate([ref[1024 + 512 * at : 1536 + 512 * at] for at in pair], axis=1) for pair in ((0, 1), (2, 3))]
     return dict(
-        along=two_parts(along).reshape(2 * pairs * points, pairs * points),
-        back=two_parts(along[picks]).reshape(2 * pairs * points, pairs * points),
-        spread=spread.astype(ml_dtypes.bfloat16),
-        quarters=two_parts(quarters),
-        halves=two_parts(halves),
-        odd=two_parts(odd),
+        quarters=(ref[0:256], ref[256:512]),
+        halves=(ref[512:768], ref[768:1024]),
+        odd=big,
+        along=ref[3072 : 3072 + 2 * side, :side],
+        back=ref[3072 : 3072 + 2 * side, side : 2 * side],
+        spread=ref[3072 + 2 * side : 3072 + 3 * side, : own * points],
     )
-
-
-NAMES = ("along", "back", "spread", "quarters", "halves", "odd")
 
 
 def split(value):
@@ -157,13 +169,12 @@
     return jnp.concatenate(columns, axis=1)
 
 
-def pair_terms(mine, partner, mine_weight, partner_weight, kernel, table):
+def pair_terms(mine, partner, mine_weight, partner_weight, modal, table):
     own, points, cells = mine.shape
     pairs = own * own
     block = cells // 4
     left = mine.astype(jnp.float32)
     right = partner.astype(jnp.float32)
-    modal = in_mode_order(kernel, points)
     along, back, spread = table["along"], table["back"], table["spread"]
     parts = []
     for at in range(4):
@@ -223,59 +234,72 @@
     return jnp.concatenate(pulled, axis=1), energy
 
 
-def weights_of(occupation_ref, owner, own):
-    return [occupation_ref[owner * own + at] for at in range(own)]
-
-
-def whereabouts(steps_ref):
+def whereabouts():
     zh, zl, core = lax.axis_index("zh"), lax.axis_index("zl"), lax.axis_index("core")
     here = lax.axis_index("y") * SIZES[2] + lax.axis_index("x")
     column = SIZES[1] * SIZES[2]
-    chip = jnp.where(zh == 0, zl, SIZES[3] - 1 - zl)
-    step = steps_ref[chip * SIZES[4] + core]
+    slot = jnp.where(zh == 0, zl, SIZES[3] - 1 - zl) * SIZES[4] + core
+    step = jnp.int32(0)
+    for at, (dy, dx) in enumerate(pair for chip in STEPS for pair in chip):
+        step = jnp.where(slot == at, dy * SIZES[2] + dx, step)
     there = jnp.bitwise_xor(here, step)
-    return core, step, zh * column + here, zh * column + there, (1 - zh) * column + there
-
-
-def first_body(steps_ref, occupation_ref, mine_ref, partner_ref, kernel_ref, *refs):
-    table = {name: ref[...] for name, ref in zip(NAMES, refs)}
-    exchange_ref, energy_ref = refs[len(NAMES) :]
-    own = mine_ref.shape[0]
-    _, _, owner, near, _ = whereabouts(steps_ref)
+    return step, zh * column + here, zh * column + there, (1 - zh) * column + there
+
+
+def prep_body(occupation_ref, kernel_ref, modal_ref, notes_ref):
+    step, *owners = whereabouts()
+    lane = lax.broadcasted_iota(jnp.int32, (1, notes_ref.shape[1]), 1)
+    row = 0
+    for owner in owners:
+        for at in range(2):
+            notes_ref[row : row + 1] = jnp.full(lane.shape, occupation_ref[owner * 2 + at])
+            row += 1
+    notes_ref[row : row + 1] = jnp.where(lane == step, 1.0, 0.0)
+    notes_ref[row + 1 : row + 2] = jnp.where(lane == SIZES[1] * SIZES[2] + step, 2.0, 0.0)
+    modal_ref[...] = in_mode_order(kernel_ref[...], kernel_ref.shape[0])
+
+
+def weights_of(notes_ref, which, own):
+    return [notes_ref[which * own + at : which * own + at + 1, 0:1] for at in range(own)]
+
+
+def first_body(partner_ref, mine_ref, table_ref, modal_ref, notes_ref, exchange_ref, energy_ref):
+    own, points, _ = mine_ref.shape
+    table = unpacked(table_ref, own, points)
     exchange, energy = pair_terms(
         mine_ref[...],
         partner_ref[...],
-        weights_of(occupation_ref, owner, own),
-        weights_of(occupation_ref, near, own),
-        kernel_ref[...],
+        weights_of(notes_ref, 0, own),
+        weights_of(notes_ref, 1, own),
+        modal_ref[...],
         table,
     )
     exchange_ref[...] = exchange
     energy_ref[...] = jnp.full(energy_ref.shape, jnp.sum(energy))
 
 
-def second_body(steps_ref, occupation_ref, mine_ref, partner_ref, kernel_ref, *refs):
-    table = {name: ref[...] for name, ref in zip(NAMES, refs)}
-    before_ref, near_ref, across_ref, keep_ref, send_ref, energy_ref = refs[len(NAMES) :]
-    own = mine_ref.shape[0]
-    core, step, owner, _, far = whereabouts(steps_ref)
+def second_body(
+    partner_ref, mine_ref, table_ref, modal_ref, notes_ref, before_ref, near_ref, across_ref, keep_ref, send_ref, energy_ref
+):
+    own, points, _ = mine_ref.shape
+    table = unpacked(table_ref, own, points)
     exchange, energy = pair_terms(
         mine_ref[...],
         partner_ref[...],
-        weights_of(occupation_ref, owner, own),
-        weights_of(occupation_ref, far, own),
-        kernel_ref[...],
+        weights_of(notes_ref, 0, own),
+        weights_of(notes_ref, 2, own),
+        modal_ref[...],
         table,
     )
     exchange = exchange + before_ref[...]
     half = exchange.shape[0] // 2
     low, high = exchange[:half], exchange[half:]
+    core = lax.axis_index("core")
     keep_ref[...] = jnp.where(core == 0, low, high)
     send_ref[...] = jnp.where(core == 0, high, low)
-    lane = lax.broadcasted_iota(jnp.int32, near_ref.shape, 1)
-    near_total = near_ref[...] + across_ref[...]
-    far_total = jnp.full(near_ref.shape, 2.0 * jnp.sum(energy))
-    row = jnp.where(lane == step, near_total, jnp.where(lane == SIZES[1] * SIZES[2] + step, far_total, 0.0))
+    near_row = notes_ref[3 * own : 3 * own + 1]
+    far_row = notes_ref[3 * own + 1 : 3 * own + 2]
+    row = (near_ref[...] + across_ref[...]) * near_row + jnp.sum(energy) * far_row
     energy_ref[...] = jnp.broadcast_to(row[None], energy_ref.shape)
 
 
@@ -336,9 +360,17 @@
     near = lax.ppermute(orbitals, AXES, routes(same_half))
     far = lax.ppermute(orbitals, AXES, routes(other_half))
 
-    table = tables(points, own, groups, cores)
-    steps = jnp.asarray(np.array([dy * SIZES[2] + dx for chip in STEPS for dy, dx in chip], np.int32))
-    constants = [jnp.asarray(table[name]) for name in NAMES]
+    table = jnp.asarray(tables(points, own, groups, cores))
+    modal, notes = pl.pallas_call(
+        prep_body,
+        out_shape=(floats(points, cells), floats(8, 128)),
+        in_specs=in_smem(1) + in_vmem(1),
+        out_specs=tuple(in_vmem(2)),
+        cost_estimate=pl.CostEstimate(flops=1 << 30, bytes_accessed=4 << 20, transcendentals=0),
+        compiler_params=PARAMS,
+        name="prep",
+    )(occupations, kernel)
+    ready = (orbitals, table, modal, notes)
     rows = own * points
     each = rows // 2 // chips
     flops = 2 * 3 * own * own * points * cells * (own * own * points + 384) * 2
@@ -346,22 +378,22 @@
     exchange, energy = pl.pallas_call(
         first_body,
         out_shape=(floats(rows, cells), floats(1, 128)),
-        in_specs=in_smem(2) + in_vmem(3 + len(NAMES)),
+        in_specs=in_vmem(1 + len(ready)),
         out_specs=tuple(in_vmem(2)),
         cost_estimate=cost,
         compiler_params=PARAMS,
         name="near_pairs",
-    )(steps, occupations, orbitals, near, kernel, *constants)
+    )(near, *ready)
     across = lax.ppermute(energy, AXES, routes(mirror))
     keep, send, energies = pl.pallas_call(
         second_body,
         out_shape=(floats(rows // 2, cells), floats(rows // 2, cells), floats(column * cores, 1, 128)),
-        in_specs=in_smem(2) + in_vmem(6 + len(NAMES)),
+        in_specs=in_vmem(4 + len(ready)),
         out_specs=tuple(in_vmem(3)),
         cost_estimate=cost,
         compiler_params=PARAMS,
         name="far_pairs",
-    )(steps, occupations, orbitals, far, kernel, *constants, exchange, energy, across)
+    )(far, *ready, exchange, energy, across)
 
     everyone = lax.all_to_all(energies, ("y", "x", "core"), 0, 0, tiled=True)
     received = lax.ppermute(send, AXES, routes(other_core))

time: 78.4 us -> 71.4 us (0.911)
  local copies, waits for them, and re-layouts: 8.69 us -> 2.42 us
  starting transfers between devices: 24.7 us -> 22.5 us
  waiting for transfers between devices: 4.1 us -> 6.23 us
    unnamed x28 -> x10, local copies, waits for them, and re-layouts: 8.69 us -> 2.42 us
    ppermute x1, waiting for transfers between devices: 0.01 us -> 2.94 us  [on_device(): far = lax.ppermute(orbitals, AXES, routes(other_half))]
    ppermute x1, starting transfers between devices: 4.36 us -> 2.24 us  [on_device(): across = lax.ppermute(energy, AXES, routes(mirror))]
    ppermute x1, waiting for transfers between devices: 4.09 us -> 3.29 us  [on_device(): across = lax.ppermute(energy, AXES, routes(mirror))]
  transfers between devices with their start and end apart: 4 -> 4, of which waited for: 1 -> 2; matrix products, arithmetic and copies ran while one was open for 0% -> 0% of each run, Pallas kernels for 3% -> 3%
where the time goes in v2:
time: 71.4 us; the launch traced here: 71.1 us
  blocking collectives  33.8 us (47%)
  starting transfers between devices  22.5 us (32%)
  waiting for transfers between devices  6.23 us (9%)
  Pallas kernels  5.38 us (8%)
  local copies, waits for them, and re-layouts  2.42 us (3%)
    all_to_all x1, blocking collectives, on_device(): pieces = lax.all_to_all(joined, 'zl', 0, 0, tiled=True)  19.4 us
    all_to_all x1, blocking collectives, on_device(): everyone = lax.all_to_all(energies, ('y', 'x', 'core'), 0, 0, tiled=True)  14.3 us
    ppermute x1, starting transfers between devices, on_device(): far = lax.ppermute(orbitals, AXES, routes(other_half))  11.1 us
    ppermute x1, starting transfers between devices, on_device(): near = lax.ppermute(orbitals, AXES, routes(same_half))  7.3 us
    ppermute x1, waiting for transfers between devices, on_device(): across = lax.ppermute(energy, AXES, routes(mirror))  3.29 us
    ppermute x1, waiting for transfers between devices, on_device(): far = lax.ppermute(orbitals, AXES, routes(other_half))  2.94 us
    unnamed x10, local copies, waits for them, and re-layouts  2.42 us
    ppermute x1, starting transfers between devices, on_device(): across = lax.ppermute(energy, AXES, routes(mirror))  2.24 us
  transfers between devices with their start and end apart: 4, of which 2 were waited for; matrix products, arithmetic and copies ran while one was open for 0% of the time, Pallas kernels for 3%

profile of v2, /device:TPU:32, one launch (start us, length us, event | category | flops | bytes accessed | tf_op | source)
XLA Modules:
  0.0 71.1 jit_solution(10906787101254261796)
XLA Ops:
  0.6 7.3 %collective-permute-start.1 = (bf16[2,32,1024]{2,1,0:T(8,128)(2,1)}, bf16[2,32,1024]{2,1,0:T(8,128)(2,1)S(1)}, u32[]{:S(2)}, u32[]{:S(2)}) collective-permute-start(bf16[2,32,1024]{2,1,0:T(8,128)(2,1)} %mine_ref.3), channel_id=1, source_target_pairs={{0,160},{1,145},{2,178},{3,227},{4,244},{5,213},{6,6},{7,71},{8,24... | collective-permute-start | bytes 393224 | tf_op jit(solution)/shard_map/ppermute | solution.py:360
  7.9 11.1 %collective-permute-start = (bf16[2,32,1024]{2,1,0:T(8,128)(2,1)}, bf16[2,32,1024]{2,1,0:T(8,128)(2,1)S(1)}, u32[]{:S(2)}, u32[]{:S(2)}) collective-permute-start(bf16[2,32,1024]{2,1,0:T(8,128)(2,1)} %mine_ref.3), channel_id=1, source_target_pairs={{0,430},{1,415},{2,444},{3,493},{4,506},{5,475},{6,264},{7,329},{8... | collective-permute-start | bytes 393224 | tf_op jit(solution)/shard_map/ppermute | solution.py:361
  19.0 0.0 copy-start.1
  19.0 0.9 %copy-done.1 = f32[32,1024]{1,0:T(8,128)S(1)} copy-done((f32[32,1024]{1,0:T(8,128)S(1)}, f32[32,1024]{1,0:T(8,128)}, u32[]{:S(2)}) %copy-start.1) | copy-done | bytes 131096
  19.9 0.0 copy-start.3
  19.9 0.7 copy-done.3
  20.6 0.0 copy-start.2
  20.6 0.0 copy-start.4
  20.6 0.7 prep.1
  21.3 0.0 collective-permute-done.1.partner_ref
  21.3 0.2 copy-done.2
  21.5 0.6 copy-done.4
  22.1 1.7 %near_pairs.1 = (f32[64,1024]{1,0:T(8,128)S(1)}, f32[1,128]{1,0:T(1,128)S(1)}) custom-call(bf16[2,32,1024]{2,1,0:T(8,128)(2,1)S(1)} %collective-permute-done.1.partner_ref, bf16[2,32,1024]{2,1,0:T(8,128)(2,1)S(1)} %copy-done.2, bf16[3456,256]{1,0:T(8,128)(2,1)S(1)} %copy-done.4, f32[32,1024]{1,0:T(8,128)S(1)} %get-tuple-element.9.modal_ref, ...), custom_call_target="tpu_custom_call" | custom-call | flops 805306368 | bytes 4194304 | tf_op jit(solution)/shard_map/near_pairs/pallas_call | solution.py:378
  23.9 2.2 %collective-permute-start.2 = (f32[1,128]{1,0:T(1,128)S(1)}, f32[1,128]{1,0:T(1,128)S(1)}, u32[]{:S(2)}, u32[]{:S(2)}) collective-permute-start(f32[1,128]{1,0:T(1,128)S(1)} %get-tuple-element.12.near_ref), channel_id=1, source_target_pairs={{0,270},{1,271},{2,268},{3,269},{4,266},{5,267},{6,264},{7,265},{8... | collective-permute-start | bytes 1544 | tf_op jit(solution)/shard_map/ppermute | solution.py:387
  26.1 2.9 %collective-permute-done.partner_ref = bf16[2,32,1024]{2,1,0:T(8,128)(2,1)S(1)} collective-permute-done((bf16[2,32,1024]{2,1,0:T(8,128)(2,1)}, bf16[2,32,1024]{2,1,0:T(8,128)(2,1)S(1)}, u32[]{:S(2)}, u32[]{:S(2)}) %collective-permute-start) | collective-permute-done | bytes 131104 | tf_op jit(solution)/shard_map/ppermute | solution.py:361
  29.1 3.3 %collective-permute-done.2.across_ref = f32[1,128]{1,0:T(1,128)S(1)} collective-permute-done((f32[1,128]{1,0:T(1,128)S(1)}, f32[1,128]{1,0:T(1,128)S(1)}, u32[]{:S(2)}, u32[]{:S(2)}) %collective-permute-start.2) | collective-permute-done | bytes 544 | tf_op jit(solution)/shard_map/ppermute | solution.py:387
  32.4 0.0 copy-start
  32.4 1.7 %far_pairs.1 = (f32[32,1024]{1,0:T(8,128)S(1)}, f32[32,1024]{1,0:T(8,128)S(1)}, f32[32,1,128]{2,1,0:T(1,128)S(1)}) custom-call(bf16[2,32,1024]{2,1,0:T(8,128)(2,1)S(1)} %collective-permute-done.partner_ref, bf16[2,32,1024]{2,1,0:T(8,128)(2,1)S(1)} %copy-done.2, bf16[3456,256]{1,0:T(8,128)(2,1)S(1)} %copy-done.4, f32[32,1024]{1,0:T(8,128)S(1)} %get-tuple-element.9.modal_ref, ...), custom_call_target="tpu_custom_call" | custom-call | flops 805306368 | bytes 4194304 | tf_op jit(solution)/shard_map/far_pairs/pallas_call | solution.py:388
  34.1 1.9 %collective-permute-start.3 = (f32[32,1024]{1,0:T(8,128)S(1)}, f32[32,1024]{1,0:T(8,128)S(1)}, u32[]{:S(2)}, u32[]{:S(2)}) collective-permute-start(f32[32,1024]{1,0:T(8,128)S(1)} %get-tuple-element.14), channel_id=1, source_target_pairs={{0,1},{1,0},{2,3},{3,2},{4,5},{5,4},{6,7},{7,6},{8,9},{9,8},{10,11... | collective-permute-start | bytes 393224 | tf_op jit(solution)/shard_map/ppermute | solution.py:399
  36.0 14.3 %all_to_all.10.energies_ref = f32[32,1,128]{2,1,0:T(1,128)S(1)} all-to-all(f32[32,1,128]{2,1,0:T(1,128)S(1)} %get-tuple-element.15), channel_id=1, replica_groups=mesh['zh'=2,'y'=4,'x'=4,'zl'=8,'core'=2] {'y','x','core'}, dimensions={0} | all-to-all | bytes 32768 | tf_op jit(solution)/shard_map/all_to_all | solution.py:398
  50.4 0.0 collective-permute-done.3.received_ref
  50.4 19.4 %all_to_all.11.pieces_ref = f32[8,4,1152]{2,1,0:T(4,128)S(1)} all-to-all(f32[8,4,1152]{2,1,0:T(4,128)S(1)} %join.1), channel_id=1, replica_groups=mesh['zh'=2,'y'=4,'x'=4,'zl'=8,'core'=2] {'zl'}, dimensions={0} | all-to-all | bytes 294912 | tf_op jit(solution)/shard_map/all_to_all | solution.py:408
  69.9 0.0 copy-done
  69.9 1.2 %last.1 = (f32[2,2,1024]{2,1,0:T(2,128)}, f32[2]{0:T(128)}) custom-call(s32[32]{0:T(128)S(1)} %copy-done, f32[8,4,1152]{2,1,0:T(4,128)S(1)} %all_to_all.11.pieces_ref), custom_call_target="tpu_custom_call" | custom-call | tf_op jit(solution)/shard_map/last/pallas_call | solution.py:409
  (1 shorter events, 0.0 us)
Async XLA Ops:
  0.6 20.6 %collective-permute-start.1 = (bf16[2,32,1024]{2,1,0:T(8,128)(2,1)}, bf16[2,32,1024]{2,1,0:T(8,128)(2,1)S(1)}, u32[]{:S(2)}, u32[]{:S(2)}) collective-permute-start(bf16[2,32,1024]{2,1,0:T(8,128)(2,1)} %mine_ref.3), channel_id=1, source_target_pairs={{0,160},{1,145},{2,178},{3,227},{4,244},{5,213},{6,6},{7,71},{8,24... | collective-permute-start | bytes 393224 | tf_op jit(solution)/shard_map/ppermute | solution.py:360
  7.9 21.1 %collective-permute-start = (bf16[2,32,1024]{2,1,0:T(8,128)(2,1)}, bf16[2,32,1024]{2,1,0:T(8,128)(2,1)S(1)}, u32[]{:S(2)}, u32[]{:S(2)}) collective-permute-start(bf16[2,32,1024]{2,1,0:T(8,128)(2,1)} %mine_ref.3), channel_id=1, source_target_pairs={{0,430},{1,415},{2,444},{3,493},{4,506},{5,475},{6,264},{7,329},{8... | collective-permute-start | bytes 393224 | tf_op jit(solution)/shard_map/ppermute | solution.py:361
  19.0 0.9 %copy-start.1 = (f32[32,1024]{1,0:T(8,128)S(1)}, f32[32,1024]{1,0:T(8,128)}, u32[]{:S(2)}) copy-start(f32[32,1024]{1,0:T(8,128)} %kernel_ref.1) | copy-start | bytes 393220
  19.9 0.7 copy-start.3
  20.6 0.9 %copy-start.2 = (bf16[2,32,1024]{2,1,0:T(8,128)(2,1)S(1)}, bf16[2,32,1024]{2,1,0:T(8,128)(2,1)}, u32[]{:S(2)}) copy-start(bf16[2,32,1024]{2,1,0:T(8,128)(2,1)} %mine_ref.3) | copy-start | bytes 393220
  20.6 1.6 %copy-start.4 = (bf16[3456,256]{1,0:T(8,128)(2,1)S(1)}, bf16[3456,256]{1,0:T(8,128)(2,1)}, u32[]{:S(2)}) copy-start(bf16[3456,256]{1,0:T(8,128)(2,1)} %constant.2.clone.table_ref) | copy-start | bytes 5308420
  23.9 8.5 %collective-permute-start.2 = (f32[1,128]{1,0:T(1,128)S(1)}, f32[1,128]{1,0:T(1,128)S(1)}, u32[]{:S(2)}, u32[]{:S(2)}) collective-permute-start(f32[1,128]{1,0:T(1,128)S(1)} %get-tuple-element.12.near_ref), channel_id=1, source_target_pairs={{0,270},{1,271},{2,268},{3,269},{4,266},{5,267},{6,264},{7,265},{8... | collective-permute-start | bytes 1544 | tf_op jit(solution)/shard_map/ppermute | solution.py:387
  32.4 37.5 %copy-start = (s32[32]{0:T(128)S(1)}, s32[32]{0:T(128)}, u32[]{:S(2)}) copy-start(s32[32]{0:T(128)} %plan_ref.1) | copy-start | bytes 388
  34.1 16.3 %collective-permute-start.3 = (f32[32,1024]{1,0:T(8,128)S(1)}, f32[32,1024]{1,0:T(8,128)S(1)}, u32[]{:S(2)}, u32[]{:S(2)}) collective-permute-start(f32[32,1024]{1,0:T(8,128)S(1)} %get-tuple-element.14), channel_id=1, source_target_pairs={{0,1},{1,0},{2,3},{3,2},{4,5},{5,4},{6,7},{7,6},{8,9},{9,8},{10,11... | collective-permute-start | bytes 393224 | tf_op jit(solution)/shard_map/ppermute | solution.py:399

commit v3 on v2

--- a/solution.py
+++ b/solution.py
@@ -169,13 +169,13 @@
     return jnp.concatenate(columns, axis=1)
 
 
-def pair_terms(mine, partner, mine_weight, partner_weight, modal, table):
+def forward(mine, partner, mine_weight, partner_weight, modal, table):
     own, points, cells = mine.shape
     pairs = own * own
     block = cells // 4
     left = mine.astype(jnp.float32)
     right = partner.astype(jnp.float32)
-    along, back, spread = table["along"], table["back"], table["spread"]
+    along = table["along"]
     parts = []
     for at in range(4):
         lanes = slice(at * block, (at + 1) * block)
@@ -212,26 +212,31 @@
             else:
                 crossed = crossed + term
     energy = straight + crossed
-    shaped = jnp.concatenate(shaped, axis=0)
+    return jnp.concatenate(shaped, axis=0), energy
+
+
+def backward(shaped, partners, weights, table):
+    own, points, cells = partners[0].shape
+    block = cells // 4
+    rows = own * points
     quarters = on_rows(shaped[:, :block], table["quarters"], 1)
     halves = on_rows(shaped[:, block : 2 * block], table["halves"], 1)
     odd = on_rows(shaped[:, 2 * block :], table["odd"], 1)
     even0, even1 = quarters + halves, quarters - halves
     odd0, odd1 = odd[:, :block], odd[:, block:]
     fields = [even0 + odd0, even1 + odd1, even0 - odd0, even1 - odd1]
-    flat = partner.reshape(own * points, cells)
-    rows = own * points
     pulled = []
     for at in range(4):
-        potential = on_planes(back, fields[at])
-        spreads = product(spread, flat[:, at * block : (at + 1) * block], ((1,), (0,)))
         total = None
-        for b in range(own):
-            term = potential[b * rows : (b + 1) * rows] * spreads[b * rows : (b + 1) * rows]
-            term = term * partner_weight[b]
-            total = term if total is None else total + term
+        for turn, (partner, weight) in enumerate(zip(partners, weights)):
+            potential = on_planes(table["back"], fields[at][turn * own * rows : (turn + 1) * own * rows])
+            flat = partner.reshape(own * points, cells)[:, at * block : (at + 1) * block]
+            spreads = product(table["spread"], flat, ((1,), (0,)))
+            for b in range(own):
+                term = potential[b * rows : (b + 1) * rows] * spreads[b * rows : (b + 1) * rows] * weight[b]
+                total = term if total is None else total + term
         pulled.append(-total)
-    return jnp.concatenate(pulled, axis=1), energy
+    return jnp.concatenate(pulled, axis=1)
 
 
 def whereabouts():
@@ -246,61 +251,56 @@
     return step, zh * column + here, zh * column + there, (1 - zh) * column + there
 
 
-def prep_body(occupation_ref, kernel_ref, modal_ref, notes_ref):
+def prep_body(occupation_ref, plan_ref, notes_ref):
     step, *owners = whereabouts()
     lane = lax.broadcasted_iota(jnp.int32, (1, notes_ref.shape[1]), 1)
-    row = 0
-    for owner in owners:
-        for at in range(2):
-            notes_ref[row : row + 1] = jnp.full(lane.shape, occupation_ref[owner * 2 + at])
-            row += 1
-    notes_ref[row : row + 1] = jnp.where(lane == step, 1.0, 0.0)
-    notes_ref[row + 1 : row + 2] = jnp.where(lane == SIZES[1] * SIZES[2] + step, 2.0, 0.0)
-    modal_ref[...] = in_mode_order(kernel_ref[...], kernel_ref.shape[0])
+    group = lax.axis_index("zl") * SIZES[4] + lax.axis_index("core")
+    rows = [jnp.full(lane.shape, occupation_ref[owner * 2 + at]) for owner in owners for at in range(2)]
+    levels = [step, SIZES[1] * SIZES[2] + step, plan_ref[group * 2], plan_ref[group * 2 + 1]]
+    rows += [jnp.where(lane == level, 1.0, 0.0) for level in levels]
+    for at, row in enumerate(rows):
+        notes_ref[at : at + 1] = row
 
 
 def weights_of(notes_ref, which, own):
     return [notes_ref[which * own + at : which * own + at + 1, 0:1] for at in range(own)]
 
 
-def first_body(partner_ref, mine_ref, table_ref, modal_ref, notes_ref, exchange_ref, energy_ref):
+NEAR, FAR = 1, 2
+
+
+def forward_body(which, partner_ref, mine_ref, table_ref, kernel_ref, notes_ref, shaped_ref, energy_ref):
     own, points, _ = mine_ref.shape
-    table = unpacked(table_ref, own, points)
-    exchange, energy = pair_terms(
+    shaped, energy = forward(
         mine_ref[...],
         partner_ref[...],
         weights_of(notes_ref, 0, own),
-        weights_of(notes_ref, 1, own),
-        modal_ref[...],
-        table,
-    )
-    exchange_ref[...] = exchange
+        weights_of(notes_ref, which, own),
+        in_mode_order(kernel_ref[...], points),
+        unpacked(table_ref, own, points),
+    )
+    shaped_ref[...] = shaped
     energy_ref[...] = jnp.full(energy_ref.shape, jnp.sum(energy))
 
 
-def second_body(
-    partner_ref, mine_ref, table_ref, modal_ref, notes_ref, before_ref, near_ref, across_ref, keep_ref, send_ref, energy_ref
-):
-    own, points, _ = mine_ref.shape
-    table = unpacked(table_ref, own, points)
-    exchange, energy = pair_terms(
-        mine_ref[...],
-        partner_ref[...],
-        weights_of(notes_ref, 0, own),
-        weights_of(notes_ref, 2, own),
-        modal_ref[...],
-        table,
-    )
-    exchange = exchange + before_ref[...]
+def back_body(near_ref, far_ref, table_ref, notes_ref, near_shaped_ref, far_shaped_ref, keep_ref, send_ref):
+    own, points, _ = near_ref.shape
+    exchange = backward(
+        jnp.concatenate([near_shaped_ref[...], far_shaped_ref[...]], axis=0),
+        [near_ref[...], far_ref[...]],
+        [weights_of(notes_ref, which, own) for which in (NEAR, FAR)],
+        unpacked(table_ref, own, points),
+    )
     half = exchange.shape[0] // 2
     low, high = exchange[:half], exchange[half:]
     core = lax.axis_index("core")
     keep_ref[...] = jnp.where(core == 0, low, high)
     send_ref[...] = jnp.where(core == 0, high, low)
-    near_row = notes_ref[3 * own : 3 * own + 1]
-    far_row = notes_ref[3 * own + 1 : 3 * own + 2]
-    row = (near_ref[...] + across_ref[...]) * near_row + jnp.sum(energy) * far_row
-    energy_ref[...] = jnp.broadcast_to(row[None], energy_ref.shape)
+
+
+def rows_body(near_ref, across_ref, far_ref, notes_ref, out_ref):
+    row = (near_ref[...] + across_ref[...]) * notes_ref[6:7] + 2.0 * far_ref[...] * notes_ref[7:8]
+    out_ref[...] = jnp.broadcast_to(row[None], out_ref.shape)
 
 
 def join_body(keep_ref, received_ref, energies_ref, out_ref):
@@ -316,8 +316,8 @@
     out_ref[:, :, cells:] = jnp.broadcast_to(rows[None, :each], (chips, each, width - cells))
 
 
-def last_body(scale, plan_ref, pieces_ref, exchange_ref, slot_ref):
-    chips, each, width = pieces_ref.shape
+def last_body(scale, notes_ref, pieces_ref, exchange_ref, slot_ref):
+    chips, _, _ = pieces_ref.shape
     own, planes, cells = exchange_ref.shape
     total = pieces_ref[0]
     for chip in range(1, chips):
@@ -325,12 +325,8 @@
     for a in range(own):
         exchange_ref[a] = total[a * planes : (a + 1) * planes, :cells]
     levels = total[:1, cells:]
-    lane = lax.broadcasted_iota(jnp.int32, levels.shape, 1)
-    slots = slot_ref.shape[0]
-    group = lax.axis_index("zl") * SIZES[4] + lax.axis_index("core")
-    for slot in range(slots):
-        level = plan_ref[group * slots + slot]
-        slot_ref[slot] = jnp.sum(jnp.where(lane == level, levels, 0.0)) * scale
+    for slot in range(slot_ref.shape[0]):
+        slot_ref[slot] = jnp.sum(levels * notes_ref[8 + slot : 9 + slot]) * scale
 
 
 def in_vmem(count):
@@ -361,63 +357,47 @@
     far = lax.ppermute(orbitals, AXES, routes(other_half))
 
     table = jnp.asarray(tables(points, own, groups, cores))
-    modal, notes = pl.pallas_call(
-        prep_body,
-        out_shape=(floats(points, cells), floats(8, 128)),
-        in_specs=in_smem(1) + in_vmem(1),
-        out_specs=tuple(in_vmem(2)),
-        cost_estimate=pl.CostEstimate(flops=1 << 30, bytes_accessed=4 << 20, transcendentals=0),
-        compiler_params=PARAMS,
-        name="prep",
-    )(occupations, kernel)
-    ready = (orbitals, table, modal, notes)
     rows = own * points
     each = rows // 2 // chips
-    flops = 2 * 3 * own * own * points * cells * (own * own * points + 384) * 2
-    cost = pl.CostEstimate(flops=flops, bytes_accessed=4 << 20, transcendentals=0)
-    exchange, energy = pl.pallas_call(
-        first_body,
-        out_shape=(floats(rows, cells), floats(1, 128)),
-        in_specs=in_vmem(1 + len(ready)),
-        out_specs=tuple(in_vmem(2)),
-        cost_estimate=cost,
-        compiler_params=PARAMS,
-        name="near_pairs",
-    )(near, *ready)
-    across = lax.ppermute(energy, AXES, routes(mirror))
-    keep, send, energies = pl.pallas_call(
-        second_body,
-        out_shape=(floats(rows // 2, cells), floats(rows // 2, cells), floats(column * cores, 1, 128)),
-        in_specs=in_vmem(4 + len(ready)),
-        out_specs=tuple(in_vmem(3)),
-        cost_estimate=cost,
-        compiler_params=PARAMS,
-        name="far_pairs",
-    )(far, *ready, exchange, energy, across)
-
+    pairs = own * own
+
+    def call(body, out_shape, *arrays, smem=0, smem_out=0, flops=0):
+        count = len(out_shape) if isinstance(out_shape, tuple) else 0
+        outs = in_vmem(max(count, 1) - smem_out) + in_smem(smem_out)
+        return pl.pallas_call(
+            body,
+            out_shape=out_shape,
+            in_specs=in_smem(smem) + in_vmem(len(arrays) - smem),
+            out_specs=tuple(outs) if count else outs[0],
+            cost_estimate=pl.CostEstimate(flops=flops, bytes_accessed=1 << 20, transcendentals=0),
+            compiler_params=PARAMS,
+        )(*arrays)
+
+    notes = call(prep_body, floats(16, 128), occupations, plan, smem=2, flops=1 << 30)
+    spectral = (floats(pairs * points, cells), floats(1, 128))
+    work = 6 * pairs * points * cells * (pairs * points + 384)
+    near_shaped, near_energy = call(
+        functools.partial(forward_body, NEAR), spectral, near, orbitals, table, kernel, notes, flops=work
+    )
+    across = lax.ppermute(near_energy, AXES, routes(mirror))
+    far_shaped, far_energy = call(
+        functools.partial(forward_body, FAR), spectral, far, orbitals, table, kernel, notes, flops=work
+    )
+    energies = call(rows_body, floats(column * cores, 1, 128), near_energy, across, far_energy, notes)
     everyone = lax.all_to_all(energies, ("y", "x", "core"), 0, 0, tiled=True)
+    half = floats(rows // 2, cells)
+    keep, send = call(back_body, (half, half), near, far, table, notes, near_shaped, far_shaped, flops=2 * work)
     received = lax.ppermute(send, AXES, routes(other_core))
-    joined = pl.pallas_call(
-        join_body,
-        out_shape=floats(chips, each, cells + 128),
-        in_specs=in_vmem(3),
-        out_specs=in_vmem(1)[0],
-        compiler_params=PARAMS,
-        name="join",
-    )(keep, received, everyone)
+    joined = call(join_body, floats(chips, each, cells + 128), keep, received, everyone)
     pieces = lax.all_to_all(joined, "zl", 0, 0, tiled=True)
-    return pl.pallas_call(
-        functools.partial(last_body, -1.0 / (2.0 * total_orbitals * points**3)),
-        out_shape=(floats(own, each // own, cells), floats(slots)),
-        in_specs=in_smem(1) + in_vmem(1),
-        out_specs=(in_vmem(1)[0], in_smem(1)[0]),
-        compiler_params=PARAMS,
-        name="last",
-    )(plan, pieces)
+    scale = -1.0 / (2.0 * total_orbitals * points**3)
+    outs = (floats(own, each // own, cells), floats(slots))
+    return call(functools.partial(last_body, scale), outs, notes, pieces, smem_out=1)
 
 
 def solution(mesh):
     split_mesh = Mesh(mesh.devices.reshape(SIZES), AXES)
+
     return jax.shard_map(
         on_device,
         mesh=split_mesh,

time: 71.4 us -> 74.5 us (1.043)
  starting transfers between devices: 22.5 us -> 29.7 us
  blocking collectives: 33.8 us -> 29 us
  waiting for transfers between devices: 6.23 us -> 8.56 us
  local copies, waits for them, and re-layouts: 2.42 us -> 1.32 us
    ppermute x1, starting transfers between devices: 2.24 us -> 9.3 us  [on_device(): across = lax.ppermute(near_energy, AXES, routes(mirror))]
    ppermute x1, waiting for transfers between devices: 2.94 us -> 7.02 us  [on_device(): far = lax.ppermute(orbitals, AXES, routes(other_half))]
    all_to_all x1, blocking collectives: 14.3 us -> 10.3 us  [on_device(): everyone = lax.all_to_all(energies, ('y', 'x', 'core'), 0, 0, tiled=True)]
    ppermute x1, waiting for transfers between devices: 3.29 us -> 1.53 us  [on_device(): across = lax.ppermute(near_energy, AXES, routes(mirror))]
    unnamed x10, local copies, waits for them, and re-layouts: 2.42 us -> 1.32 us
    all_to_all x1, blocking collectives: 19.4 us -> 18.6 us  [on_device(): pieces = lax.all_to_all(joined, 'zl', 0, 0, tiled=True)]
    pallas_call x5 -> x7, Pallas kernels: 5.38 us -> 4.89 us  [call(): pl.pallas_call(body, out_shape=out_shape, in_specs=in_smem(smem) + in_vme...]
  transfers between devices with their start and end apart: 4 -> 4, of which waited for: 2 -> 2; matrix products, arithmetic and copies ran while one was open for 0% -> 0% of each run, Pallas kernels for 3% -> 2%
where the time goes in v3:
time: 74.5 us; the launch traced here: 74.2 us
  starting transfers between devices  29.7 us (40%)
  blocking collectives  29 us (39%)
  waiting for transfers between devices  8.56 us (11%)
  Pallas kernels  4.89 us (7%)
  local copies, waits for them, and re-layouts  1.32 us (2%)
  between operations  0.76 us (1%)
    all_to_all x1, blocking collectives, on_device(): pieces = lax.all_to_all(joined, 'zl', 0, 0, tiled=True)  18.6 us
    ppermute x1, starting transfers between devices, on_device(): far = lax.ppermute(orbitals, AXES, routes(other_half))  11.1 us
    all_to_all x1, blocking collectives, on_device(): everyone = lax.all_to_all(energies, ('y', 'x', 'core'), 0, 0, tiled=True)  10.3 us
    ppermute x1, starting transfers between devices, on_device(): across = lax.ppermute(near_energy, AXES, routes(mirror))  9.3 us
    ppermute x1, starting transfers between devices, on_device(): near = lax.ppermute(orbitals, AXES, routes(same_half))  7.43 us
    ppermute x1, waiting for transfers between devices, on_device(): far = lax.ppermute(orbitals, AXES, routes(other_half))  7.02 us
    pallas_call x7, Pallas kernels, call(): pl.pallas_call(body, out_shape=out_shape, in_specs=in_smem(smem) + in_vme...  4.89 us
    ppermute x1, starting transfers between devices, on_device(): received = lax.ppermute(send, AXES, routes(other_core))  1.92 us
  transfers between devices with their start and end apart: 4, of which 2 were waited for; matrix products, arithmetic and copies ran while one was open for 0% of the time, Pallas kernels for 2%

profile of v3, /device:TPU:32, one launch (start us, length us, event | category | flops | bytes accessed | tf_op | source)
XLA Modules:
  0.0 74.2 jit_solution(6597709037911578024)
XLA Ops:
  0.6 0.0 copy-start
  0.6 0.0 copy-start.1
  0.7 0.0 copy-start.2
  0.7 7.4 %collective-permute-start = (bf16[2,32,1024]{2,1,0:T(8,128)(2,1)}, bf16[2,32,1024]{2,1,0:T(8,128)(2,1)S(1)}, u32[]{:S(2)}, u32[]{:S(2)}) collective-permute-start(bf16[2,32,1024]{2,1,0:T(8,128)(2,1)} %mine_ref.3), channel_id=1, source_target_pairs={{0,160},{1,145},{2,178},{3,227},{4,244},{5,213},{6,6},{7,71},{8,24... | collective-permute-start | bytes 393224 | tf_op jit(solution)/shard_map/ppermute | solution.py:356
  8.1 11.1 %collective-permute-start.1 = (bf16[2,32,1024]{2,1,0:T(8,128)(2,1)}, bf16[2,32,1024]{2,1,0:T(8,128)(2,1)S(1)}, u32[]{:S(2)}, u32[]{:S(2)}) collective-permute-start(bf16[2,32,1024]{2,1,0:T(8,128)(2,1)} %mine_ref.3), channel_id=1, source_target_pairs={{0,430},{1,415},{2,444},{3,493},{4,506},{5,475},{6,264},{7,329},{8... | collective-permute-start | bytes 393224 | tf_op jit(solution)/shard_map/ppermute | solution.py:357
  19.2 0.0 copy-start.3
  19.2 0.6 copy-done.3
  19.8 0.7 copy-done.4
  20.5 0.6 shard_map.68.notes_ref
  21.1 0.0 collective-permute-done.partner_ref.near_ref
  21.1 0.0 copy-done
  21.1 0.0 copy-done.1
  21.1 0.0 copy-done.2
  21.1 1.1 %shard_map.69 = (f32[128,1024]{1,0:T(8,128)S(1)}, f32[1,128]{1,0:T(1,128)S(1)}) custom-call(bf16[2,32,1024]{2,1,0:T(8,128)(2,1)S(1)} %collective-permute-done.partner_ref.near_ref, bf16[2,32,1024]{2,1,0:T(8,128)(2,1)S(1)} %copy-done.1, bf16[3456,256]{1,0:T(8,128)(2,1)S(1)} %copy-done, f32[32,1024]{1,0:T(8,128)S(1)} %copy-done.2, ...), custom_call_target="tpu_custom_call" | custom-call | flops 402653184 | bytes 1048576 | tf_op jit(solution)/shard_map/pallas_call | solution.py:367
  22.2 7.0 %collective-permute-done.1.partner_ref.far_ref = bf16[2,32,1024]{2,1,0:T(8,128)(2,1)S(1)} collective-permute-done((bf16[2,32,1024]{2,1,0:T(8,128)(2,1)}, bf16[2,32,1024]{2,1,0:T(8,128)(2,1)S(1)}, u32[]{:S(2)}, u32[]{:S(2)}) %collective-permute-start.1) | collective-permute-done | bytes 131104 | tf_op jit(solution)/shard_map/ppermute | solution.py:357
  29.2 1.0 %shard_map.70 = (f32[128,1024]{1,0:T(8,128)S(1)}, f32[1,128]{1,0:T(1,128)S(1)}) custom-call(bf16[2,32,1024]{2,1,0:T(8,128)(2,1)S(1)} %collective-permute-done.1.partner_ref.far_ref, bf16[2,32,1024]{2,1,0:T(8,128)(2,1)S(1)} %copy-done.1, bf16[3456,256]{1,0:T(8,128)(2,1)S(1)} %copy-done, f32[32,1024]{1,0:T(8,128)S(1)} %copy-done.2, ...), custom_call_target="tpu_custom_call" | custom-call | flops 402653184 | bytes 1048576 | tf_op jit(solution)/shard_map/pallas_call | solution.py:367
  30.3 1.5 %shard_map.71 = (f32[32,1024]{1,0:T(8,128)S(1)}, f32[32,1024]{1,0:T(8,128)S(1)}) custom-call(bf16[2,32,1024]{2,1,0:T(8,128)(2,1)S(1)} %collective-permute-done.partner_ref.near_ref, bf16[2,32,1024]{2,1,0:T(8,128)(2,1)S(1)} %collective-permute-done.1.partner_ref.far_ref, bf16[3456,256]{1,0:T(8,128)(2,1)S(1)} %copy-done, f32[16,128]{1,0:T(8,128)S(1)} %shard_map.68.notes_ref, ...), custom_call_target="tpu_custom_call" | custom-call | flops 805306368 | bytes 1048576 | tf_op jit(solution)/shard_map/pallas_call | solution.py:367
  31.8 1.9 %collective-permute-start.2 = (f32[32,1024]{1,0:T(8,128)S(1)}, f32[32,1024]{1,0:T(8,128)S(1)}, u32[]{:S(2)}, u32[]{:S(2)}) collective-permute-start(f32[32,1024]{1,0:T(8,128)S(1)} %get-tuple-element.11), channel_id=1, source_target_pairs={{0,1},{1,0},{2,3},{3,2},{4,5},{5,4},{6,7},{7,6},{8,9},{9,8},{10,11... | collective-permute-start | bytes 393224 | tf_op jit(solution)/shard_map/ppermute | solution.py:390
  33.7 9.3 %collective-permute-start.3 = (f32[1,128]{1,0:T(1,128)S(1)}, f32[1,128]{1,0:T(1,128)S(1)}, u32[]{:S(2)}, u32[]{:S(2)}) collective-permute-start(f32[1,128]{1,0:T(1,128)S(1)} %get-tuple-element.12.near_ref), channel_id=1, source_target_pairs={{0,270},{1,271},{2,268},{3,269},{4,266},{5,267},{6,264},{7,265},{8... | collective-permute-start | bytes 1544 | tf_op jit(solution)/shard_map/ppermute | solution.py:382
  43.0 1.5 %collective-permute-done.3.across_ref = f32[1,128]{1,0:T(1,128)S(1)} collective-permute-done((f32[1,128]{1,0:T(1,128)S(1)}, f32[1,128]{1,0:T(1,128)S(1)}, u32[]{:S(2)}, u32[]{:S(2)}) %collective-permute-start.3) | collective-permute-done | bytes 544 | tf_op jit(solution)/shard_map/ppermute | solution.py:382
  44.6 10.3 %all_to_all.10.energies_ref = f32[32,1,128]{2,1,0:T(1,128)S(1)} all-to-all(f32[32,1,128]{2,1,0:T(1,128)S(1)} %shard_map.72), channel_id=1, replica_groups=mesh['zh'=2,'y'=4,'x'=4,'zl'=8,'core'=2] {'y','x','core'}, dimensions={0} | all-to-all | bytes 32768 | tf_op jit(solution)/shard_map/all_to_all | solution.py:387
  54.9 0.0 collective-permute-done.2.received_ref
  55.0 18.6 %all_to_all.11.pieces_ref = f32[8,4,1152]{2,1,0:T(4,128)S(1)} all-to-all(f32[8,4,1152]{2,1,0:T(4,128)S(1)} %shard_map.73), channel_id=1, replica_groups=mesh['zh'=2,'y'=4,'x'=4,'zl'=8,'core'=2] {'zl'}, dimensions={0} | all-to-all | bytes 294912 | tf_op jit(solution)/shard_map/all_to_all | solution.py:392
  73.6 0.6 shard_map.74
  (3 shorter events, 0.1 us)
Async XLA Ops:
  0.6 20.5 %copy-start = (bf16[3456,256]{1,0:T(8,128)(2,1)S(1)}, bf16[3456,256]{1,0:T(8,128)(2,1)}, u32[]{:S(2)}) copy-start(bf16[3456,256]{1,0:T(8,128)(2,1)} %constant.2.clone.table_ref) | copy-start | bytes 5308420
  0.6 20.5 %copy-start.1 = (bf16[2,32,1024]{2,1,0:T(8,128)(2,1)S(1)}, bf16[2,32,1024]{2,1,0:T(8,128)(2,1)}, u32[]{:S(2)}) copy-start(bf16[2,32,1024]{2,1,0:T(8,128)(2,1)} %mine_ref.3) | copy-start | bytes 393220
  0.7 20.5 %copy-start.2 = (f32[32,1024]{1,0:T(8,128)S(1)}, f32[32,1024]{1,0:T(8,128)}, u32[]{:S(2)}) copy-start(f32[32,1024]{1,0:T(8,128)} %kernel_ref.3) | copy-start | bytes 393220
  0.7 20.4 %collective-permute-start = (bf16[2,32,1024]{2,1,0:T(8,128)(2,1)}, bf16[2,32,1024]{2,1,0:T(8,128)(2,1)S(1)}, u32[]{:S(2)}, u32[]{:S(2)}) collective-permute-start(bf16[2,32,1024]{2,1,0:T(8,128)(2,1)} %mine_ref.3), channel_id=1, source_target_pairs={{0,160},{1,145},{2,178},{3,227},{4,244},{5,213},{6,6},{7,71},{8,24... | collective-permute-start | bytes 393224 | tf_op jit(solution)/shard_map/ppermute | solution.py:356
  8.1 21.1 %collective-permute-start.1 = (bf16[2,32,1024]{2,1,0:T(8,128)(2,1)}, bf16[2,32,1024]{2,1,0:T(8,128)(2,1)S(1)}, u32[]{:S(2)}, u32[]{:S(2)}) collective-permute-start(bf16[2,32,1024]{2,1,0:T(8,128)(2,1)} %mine_ref.3), channel_id=1, source_target_pairs={{0,430},{1,415},{2,444},{3,493},{4,506},{5,475},{6,264},{7,329},{8... | collective-permute-start | bytes 393224 | tf_op jit(solution)/shard_map/ppermute | solution.py:357
  19.2 0.7 copy-start.3
  19.8 0.7 copy-start.4
  31.8 23.1 %collective-permute-start.2 = (f32[32,1024]{1,0:T(8,128)S(1)}, f32[32,1024]{1,0:T(8,128)S(1)}, u32[]{:S(2)}, u32[]{:S(2)}) collective-permute-start(f32[32,1024]{1,0:T(8,128)S(1)} %get-tuple-element.11), channel_id=1, source_target_pairs={{0,1},{1,0},{2,3},{3,2},{4,5},{5,4},{6,7},{7,6},{8,9},{9,8},{10,11... | collective-permute-start | bytes 393224 | tf_op jit(solution)/shard_map/ppermute | solution.py:390
  33.7 10.8 %collective-permute-start.3 = (f32[1,128]{1,0:T(1,128)S(1)}, f32[1,128]{1,0:T(1,128)S(1)}, u32[]{:S(2)}, u32[]{:S(2)}) collective-permute-start(f32[1,128]{1,0:T(1,128)S(1)} %get-tuple-element.12.near_ref), channel_id=1, source_target_pairs={{0,270},{1,271},{2,268},{3,269},{4,266},{5,267},{6,264},{7,265},{8... | collective-permute-start | bytes 1544 | tf_op jit(solution)/shard_map/ppermute | solution.py:382

commit v4 on v3

--- a/solution.py
+++ b/solution.py
@@ -39,8 +39,8 @@
     return flat
 
 
-def routes(move):
-    return [(place(c), place(move(*c))) for c in np.ndindex(*SIZES)]
+def routes(move, half=None):
+    return [(place(c), place(move(*c))) for c in np.ndindex(*SIZES) if half in (None, c[0])]
 
 
 def same_half(zh, y, x, zl, core):
@@ -251,17 +251,27 @@
     return step, zh * column + here, zh * column + there, (1 - zh) * column + there
 
 
-def prep_body(occupation_ref, plan_ref, notes_ref):
+def prep_body(occupation_ref, notes_ref):
     step, *owners = whereabouts()
     lane = lax.broadcasted_iota(jnp.int32, (1, notes_ref.shape[1]), 1)
-    group = lax.axis_index("zl") * SIZES[4] + lax.axis_index("core")
     rows = [jnp.full(lane.shape, occupation_ref[owner * 2 + at]) for owner in owners for at in range(2)]
-    levels = [step, SIZES[1] * SIZES[2] + step, plan_ref[group * 2], plan_ref[group * 2 + 1]]
-    rows += [jnp.where(lane == level, 1.0, 0.0) for level in levels]
+    rows += [jnp.where(lane == level, 1.0, 0.0) for level in (step, SIZES[1] * SIZES[2] + step)]
     for at, row in enumerate(rows):
         notes_ref[at : at + 1] = row
 
 
+def picks_body(plan_ref, picks_ref):
+    slots = picks_ref.shape[0]
+    lane = lax.broadcasted_iota(jnp.int32, (1, picks_ref.shape[1]), 1)
+    group = lax.axis_index("zl") * SIZES[4] + lax.axis_index("core")
+    for slot in range(slots):
+        picks_ref[slot : slot + 1] = jnp.where(lane == plan_ref[group * slots + slot], 1.0, 0.0)
+
+
+def taken(first_ref, second_ref, first):
+    return jnp.where(first, first_ref[...], second_ref[...])
+
+
 def weights_of(notes_ref, which, own):
     return [notes_ref[which * own + at : which * own + at + 1, 0:1] for at in range(own)]
 
@@ -269,11 +279,13 @@
 NEAR, FAR = 1, 2
 
 
-def forward_body(which, partner_ref, mine_ref, table_ref, kernel_ref, notes_ref, shaped_ref, energy_ref):
+def forward_body(which, low_ref, high_ref, mine_ref, table_ref, kernel_ref, notes_ref, shaped_ref, energy_ref, partner_ref):
     own, points, _ = mine_ref.shape
+    partner = taken(low_ref, high_ref, lax.axis_index("zh") == 0)
+    partner_ref[...] = partner
     shaped, energy = forward(
         mine_ref[...],
-        partner_ref[...],
+        partner,
         weights_of(notes_ref, 0, own),
         weights_of(notes_ref, which, own),
         in_mode_order(kernel_ref[...], points),
@@ -316,7 +328,7 @@
     out_ref[:, :, cells:] = jnp.broadcast_to(rows[None, :each], (chips, each, width - cells))
 
 
-def last_body(scale, notes_ref, pieces_ref, exchange_ref, slot_ref):
+def last_body(scale, picks_ref, pieces_ref, exchange_ref, slot_ref):
     chips, _, _ = pieces_ref.shape
     own, planes, cells = exchange_ref.shape
     total = pieces_ref[0]
@@ -326,7 +338,7 @@
         exchange_ref[a] = total[a * planes : (a + 1) * planes, :cells]
     levels = total[:1, cells:]
     for slot in range(slot_ref.shape[0]):
-        slot_ref[slot] = jnp.sum(levels * notes_ref[8 + slot : 9 + slot]) * scale
+        slot_ref[slot] = jnp.sum(levels * picks_ref[slot : slot + 1]) * scale
 
 
 def in_vmem(count):
@@ -353,8 +365,11 @@
     slots = plan.shape[0] // groups
     column = lax.axis_size(("y", "x"))
 
-    near = lax.ppermute(orbitals, AXES, routes(same_half))
-    far = lax.ppermute(orbitals, AXES, routes(other_half))
+    def moved(move, half):
+        return lax.ppermute(orbitals, AXES, routes(move, half))
+
+    far = [moved(other_half, 1), moved(other_half, 0)]
+    near = [moved(same_half, 0), moved(same_half, 1)]
 
     table = jnp.asarray(tables(points, own, groups, cores))
     rows = own * points
@@ -373,15 +388,16 @@
             compiler_params=PARAMS,
         )(*arrays)
 
-    notes = call(prep_body, floats(16, 128), occupations, plan, smem=2, flops=1 << 30)
-    spectral = (floats(pairs * points, cells), floats(1, 128))
+    notes = call(prep_body, floats(8, 128), occupations, smem=1, flops=1 << 30)
+    spectral = (floats(pairs * points, cells), floats(1, 128), jax.ShapeDtypeStruct(orbitals.shape, orbitals.dtype))
     work = 6 * pairs * points * cells * (pairs * points + 384)
-    near_shaped, near_energy = call(
-        functools.partial(forward_body, NEAR), spectral, near, orbitals, table, kernel, notes, flops=work
+    near_shaped, near_energy, near = call(
+        functools.partial(forward_body, NEAR), spectral, *near, orbitals, table, kernel, notes, flops=work
     )
     across = lax.ppermute(near_energy, AXES, routes(mirror))
-    far_shaped, far_energy = call(
-        functools.partial(forward_body, FAR), spectral, far, orbitals, table, kernel, notes, flops=work
+    picks = call(picks_body, floats(slots, 128), plan, smem=1)
+    far_shaped, far_energy, far = call(
+        functools.partial(forward_body, FAR), spectral, *far, orbitals, table, kernel, notes, flops=work
     )
     energies = call(rows_body, floats(column * cores, 1, 128), near_energy, across, far_energy, notes)
     everyone = lax.all_to_all(energies, ("y", "x", "core"), 0, 0, tiled=True)
@@ -392,7 +408,7 @@
     pieces = lax.all_to_all(joined, "zl", 0, 0, tiled=True)
     scale = -1.0 / (2.0 * total_orbitals * points**3)
     outs = (floats(own, each // own, cells), floats(slots))
-    return call(functools.partial(last_body, scale), outs, notes, pieces, smem_out=1)
+    return call(functools.partial(last_body, scale), outs, picks, pieces, smem_out=1)
 
 
 def solution(mesh):

time: 74.5 us -> 78.9 us (1.059)
  blocking collectives: 29 us -> 10.3 us
  starting transfers between devices: 29.7 us -> 43.1 us
  waiting for transfers between devices: 8.56 us -> 17.5 us
  Pallas kernels: 4.89 us -> 6.1 us
    all_to_all x1 -> x0, blocking collectives: 18.6 us -> none  [on_device(): pieces = lax.all_to_all(joined, 'zl', 0, 0, tiled=True)]
    all_to_all x0 -> x1, waiting for transfers between devices: none -> 11.2 us  [on_device(): pieces = lax.all_to_all(joined, 'zl', 0, 0, tiled=True)]
    all_to_all x0 -> x1, starting transfers between devices: none -> 8.52 us  [on_device(): pieces = lax.all_to_all(joined, 'zl', 0, 0, tiled=True)]
    ppermute x2 -> x4, starting transfers between devices: 18.5 us -> 21.5 us  [moved(): return lax.ppermute(orbitals, AXES, routes(move, half))]
    ppermute x2 -> x4, waiting for transfers between devices: 7.02 us -> 4.76 us  [moved(): return lax.ppermute(orbitals, AXES, routes(move, half))]
    ppermute x1, starting transfers between devices: 9.3 us -> 11.2 us  [on_device(): across = lax.ppermute(near_energy, AXES, routes(mirror))]
    pallas_call x7 -> x8, Pallas kernels: 4.89 us -> 6.1 us  [call(): pl.pallas_call(body, out_shape=out_shape, in_specs=in_smem(smem) + in_vme...]
  transfers between devices with their start and end apart: 4 -> 7, of which waited for: 2 -> 3; matrix products, arithmetic and copies ran while one was open for 0% -> 0% of each run, Pallas kernels for 2% -> 3%
where the time goes in v4:
time: 78.9 us; the launch traced here: 78.5 us
  starting transfers between devices  43.1 us (55%)
  waiting for transfers between devices  17.5 us (22%)
  blocking collectives  10.3 us (13%)
  Pallas kernels  6.1 us (8%)
  between operations  0.8 us (1%)
    ppermute x4, starting transfers between devices, moved(): return lax.ppermute(orbitals, AXES, routes(move, half))  21.5 us
    ppermute x1, starting transfers between devices, on_device(): across = lax.ppermute(near_energy, AXES, routes(mirror))  11.2 us
    all_to_all x1, waiting for transfers between devices, on_device(): pieces = lax.all_to_all(joined, 'zl', 0, 0, tiled=True)  11.2 us
    all_to_all x1, blocking collectives, on_device(): everyone = lax.all_to_all(energies, ('y', 'x', 'core'), 0, 0, tiled=True)  10.3 us
    all_to_all x1, starting transfers between devices, on_device(): pieces = lax.all_to_all(joined, 'zl', 0, 0, tiled=True)  8.52 us
    pallas_call x8, Pallas kernels, call(): pl.pallas_call(body, out_shape=out_shape, in_specs=in_smem(smem) + in_vme...  6.1 us
    ppermute x4, waiting for transfers between devices, moved(): return lax.ppermute(orbitals, AXES, routes(move, half))  4.76 us
    ppermute x1, starting transfers between devices, on_device(): received = lax.ppermute(send, AXES, routes(other_core))  1.92 us
  transfers between devices with their start and end apart: 7, of which 3 were waited for; matrix products, arithmetic and copies ran while one was open for 0% of the time, Pallas kernels for 3%

profile of v4, /device:TPU:32, one launch (start us, length us, event | category | flops | bytes accessed | tf_op | source)
XLA Modules:
  0.0 78.5 jit_solution(1097686696203711817)
XLA Ops:
  0.6 0.0 copy-start
  0.7 7.4 %collective-permute-start = (bf16[2,32,1024]{2,1,0:T(8,128)(2,1)}, bf16[2,32,1024]{2,1,0:T(8,128)(2,1)S(1)}, u32[]{:S(2)}, u32[]{:S(2)}) collective-permute-start(bf16[2,32,1024]{2,1,0:T(8,128)(2,1)} %mine_ref.3), channel_id=1, source_target_pairs={{0,160},{1,145},{2,178},{3,227},{4,244},{5,213},{6,6},{7,71},{8,24... | collective-permute-start | bytes 393224 | tf_op jit(solution)/shard_map/ppermute | solution.py:369
  8.1 0.7 collective-permute-start.1
  8.8 1.3 %collective-permute-start.2 = (bf16[2,32,1024]{2,1,0:T(8,128)(2,1)}, bf16[2,32,1024]{2,1,0:T(8,128)(2,1)S(1)}, u32[]{:S(2)}, u32[]{:S(2)}) collective-permute-start(bf16[2,32,1024]{2,1,0:T(8,128)(2,1)} %mine_ref.3), channel_id=1, source_target_pairs={{256,110},{257,143},{258,44},{259,205},{260,122},{261,91},{262,24}... | collective-permute-start | bytes 393224 | tf_op jit(solution)/shard_map/ppermute | solution.py:369
  10.1 12.1 %collective-permute-start.3 = (bf16[2,32,1024]{2,1,0:T(8,128)(2,1)}, bf16[2,32,1024]{2,1,0:T(8,128)(2,1)S(1)}, u32[]{:S(2)}, u32[]{:S(2)}) collective-permute-start(bf16[2,32,1024]{2,1,0:T(8,128)(2,1)} %mine_ref.3), channel_id=1, source_target_pairs={{0,430},{1,415},{2,444},{3,493},{4,506},{5,475},{6,264},{7,329},{8... | collective-permute-start | bytes 393224 | tf_op jit(solution)/shard_map/ppermute | solution.py:369
  22.2 0.6 copy-done.3
  22.8 0.6 shard_map.69.notes_ref
  23.4 0.0 collective-permute-done.low_ref
  23.4 0.0 collective-permute-done.1.high_ref
  23.4 1.1 %shard_map.70 = (f32[128,1024]{1,0:T(8,128)S(1)}, f32[1,128]{1,0:T(1,128)S(1)}, bf16[2,32,1024]{2,1,0:T(8,128)(2,1)S(1)}) custom-call(bf16[2,32,1024]{2,1,0:T(8,128)(2,1)S(1)} %collective-permute-done.low_ref, bf16[2,32,1024]{2,1,0:T(8,128)(2,1)S(1)} %collective-permute-done.1.high_ref, bf16[2,32,1024]{2,1,0:T(8,128)(2,1)S(1)} %copy-done.1, ...), custom_call_target="tpu_custom_call" | custom-call | flops 402653184 | bytes 1048576 | tf_op jit(solution)/shard_map/pallas_call | solution.py:382
  24.5 4.8 %collective-permute-done.2.low_ref = bf16[2,32,1024]{2,1,0:T(8,128)(2,1)S(1)} collective-permute-done((bf16[2,32,1024]{2,1,0:T(8,128)(2,1)}, bf16[2,32,1024]{2,1,0:T(8,128)(2,1)S(1)}, u32[]{:S(2)}, u32[]{:S(2)}) %collective-permute-start.2) | collective-permute-done | bytes 131104 | tf_op jit(solution)/shard_map/ppermute | solution.py:369
  29.3 1.1 %shard_map.71 = (f32[128,1024]{1,0:T(8,128)S(1)}, f32[1,128]{1,0:T(1,128)S(1)}, bf16[2,32,1024]{2,1,0:T(8,128)(2,1)S(1)}) custom-call(bf16[2,32,1024]{2,1,0:T(8,128)(2,1)S(1)} %collective-permute-done.2.low_ref, bf16[2,32,1024]{2,1,0:T(8,128)(2,1)S(1)} %collective-permute-done.3.high_ref, bf16[2,32,1024]{2,1,0:T(8,128)(2,1)S(1)} %copy-done.1, ...), custom_call_target="tpu_custom_call" | custom-call | flops 402653184 | bytes 1048576 | tf_op jit(solution)/shard_map/pallas_call | solution.py:382
  30.3 0.0 copy-start.4
  30.4 1.5 %shard_map.72 = (f32[32,1024]{1,0:T(8,128)S(1)}, f32[32,1024]{1,0:T(8,128)S(1)}) custom-call(bf16[2,32,1024]{2,1,0:T(8,128)(2,1)S(1)} %get-tuple-element.10.near_ref, bf16[2,32,1024]{2,1,0:T(8,128)(2,1)S(1)} %get-tuple-element.11.far_ref, bf16[3456,256]{1,0:T(8,128)(2,1)S(1)} %copy-done, f32[8,128]{1,0:T(8,128)S(1)} %shard_map.69.notes_ref, ...), custom_call_target="tpu_custom_call" | custom-call | flops 805306368 | bytes 1048576 | tf_op jit(solution)/shard_map/pallas_call | solution.py:382
  31.9 1.9 %collective-permute-start.4 = (f32[32,1024]{1,0:T(8,128)S(1)}, f32[32,1024]{1,0:T(8,128)S(1)}, u32[]{:S(2)}, u32[]{:S(2)}) collective-permute-start(f32[32,1024]{1,0:T(8,128)S(1)} %get-tuple-element.15), channel_id=1, source_target_pairs={{0,1},{1,0},{2,3},{3,2},{4,5},{5,4},{6,7},{7,6},{8,9},{9,8},{10,11... | collective-permute-start | bytes 393224 | tf_op jit(solution)/shard_map/ppermute | solution.py:406
  33.8 11.2 %collective-permute-start.5 = (f32[1,128]{1,0:T(1,128)S(1)}, f32[1,128]{1,0:T(1,128)S(1)}, u32[]{:S(2)}, u32[]{:S(2)}) collective-permute-start(f32[1,128]{1,0:T(1,128)S(1)} %get-tuple-element.16.near_ref), channel_id=1, source_target_pairs={{0,270},{1,271},{2,268},{3,269},{4,266},{5,267},{6,264},{7,265},{8... | collective-permute-start | bytes 1544 | tf_op jit(solution)/shard_map/ppermute | solution.py:397
  45.0 1.5 %collective-permute-done.5.across_ref = f32[1,128]{1,0:T(1,128)S(1)} collective-permute-done((f32[1,128]{1,0:T(1,128)S(1)}, f32[1,128]{1,0:T(1,128)S(1)}, u32[]{:S(2)}, u32[]{:S(2)}) %collective-permute-start.5) | collective-permute-done | bytes 544 | tf_op jit(solution)/shard_map/ppermute | solution.py:397
  46.6 10.3 %all_to_all.10.energies_ref = f32[32,1,128]{2,1,0:T(1,128)S(1)} all-to-all(f32[32,1,128]{2,1,0:T(1,128)S(1)} %shard_map.73), channel_id=1, replica_groups=mesh['zh'=2,'y'=4,'x'=4,'zl'=8,'core'=2] {'y','x','core'}, dimensions={0} | all-to-all | bytes 32768 | tf_op jit(solution)/shard_map/all_to_all | solution.py:403
  56.9 0.0 collective-permute-done.4.received_ref
  56.9 0.7 shard_map.74
  57.6 8.5 %all-to-all-start.1 = ((f32[8,4,1152]{2,1,0:T(4,128)}), f32[8,4,1152]{2,1,0:T(4,128)S(1)}, u32[]{:S(2)}, u32[]{:S(2)}) async-start(f32[8,4,1152]{2,1,0:T(4,128)} %shard_map.74), calls=%async_computation.1 | async-start | bytes 294912 | tf_op jit(solution)/shard_map/all_to_all | solution.py:408
  66.1 0.6 shard_map.68.picks_ref
  66.7 11.2 %all-to-all-done.1.pieces_ref = f32[8,4,1152]{2,1,0:T(4,128)S(1)} async-done(((f32[8,4,1152]{2,1,0:T(4,128)}), f32[8,4,1152]{2,1,0:T(4,128)S(1)}, u32[]{:S(2)}, u32[]{:S(2)}) %all-to-all-start.1) | async-done | bytes 147488 | tf_op jit(solution)/shard_map/all_to_all | solution.py:408
  77.9 0.6 shard_map.75
  (9 shorter events, 0.0 us)
Async XLA Ops:
  0.6 22.8 %copy-start = (bf16[3456,256]{1,0:T(8,128)(2,1)S(1)}, bf16[3456,256]{1,0:T(8,128)(2,1)}, u32[]{:S(2)}) copy-start(bf16[3456,256]{1,0:T(8,128)(2,1)} %constant.2.clone.table_ref) | copy-start | bytes 5308420
  0.6 22.8 %copy-start.1 = (bf16[2,32,1024]{2,1,0:T(8,128)(2,1)S(1)}, bf16[2,32,1024]{2,1,0:T(8,128)(2,1)}, u32[]{:S(2)}) copy-start(bf16[2,32,1024]{2,1,0:T(8,128)(2,1)} %mine_ref.3) | copy-start | bytes 393220
  0.7 22.8 %copy-start.2 = (f32[32,1024]{1,0:T(8,128)S(1)}, f32[32,1024]{1,0:T(8,128)}, u32[]{:S(2)}) copy-start(f32[32,1024]{1,0:T(8,128)} %kernel_ref.3) | copy-start | bytes 393220
  0.7 22.7 %collective-permute-start = (bf16[2,32,1024]{2,1,0:T(8,128)(2,1)}, bf16[2,32,1024]{2,1,0:T(8,128)(2,1)S(1)}, u32[]{:S(2)}, u32[]{:S(2)}) collective-permute-start(bf16[2,32,1024]{2,1,0:T(8,128)(2,1)} %mine_ref.3), channel_id=1, source_target_pairs={{0,160},{1,145},{2,178},{3,227},{4,244},{5,213},{6,6},{7,71},{8,24... | collective-permute-start | bytes 393224 | tf_op jit(solution)/shard_map/ppermute | solution.py:369
  8.1 15.3 %collective-permute-start.1 = (bf16[2,32,1024]{2,1,0:T(8,128)(2,1)}, bf16[2,32,1024]{2,1,0:T(8,128)(2,1)S(1)}, u32[]{:S(2)}, u32[]{:S(2)}) collective-permute-start(bf16[2,32,1024]{2,1,0:T(8,128)(2,1)} %mine_ref.3), channel_id=1, source_target_pairs={{256,352},{257,385},{258,290},{259,451},{260,372},{261,341},{262,2... | collective-permute-start | bytes 393224 | tf_op jit(solution)/shard_map/ppermute | solution.py:369
  8.8 20.5 %collective-permute-start.2 = (bf16[2,32,1024]{2,1,0:T(8,128)(2,1)}, bf16[2,32,1024]{2,1,0:T(8,128)(2,1)S(1)}, u32[]{:S(2)}, u32[]{:S(2)}) collective-permute-start(bf16[2,32,1024]{2,1,0:T(8,128)(2,1)} %mine_ref.3), channel_id=1, source_target_pairs={{256,110},{257,143},{258,44},{259,205},{260,122},{261,91},{262,24}... | collective-permute-start | bytes 393224 | tf_op jit(solution)/shard_map/ppermute | solution.py:369
  10.1 19.2 %collective-permute-start.3 = (bf16[2,32,1024]{2,1,0:T(8,128)(2,1)}, bf16[2,32,1024]{2,1,0:T(8,128)(2,1)S(1)}, u32[]{:S(2)}, u32[]{:S(2)}) collective-permute-start(bf16[2,32,1024]{2,1,0:T(8,128)(2,1)} %mine_ref.3), channel_id=1, source_target_pairs={{0,430},{1,415},{2,444},{3,493},{4,506},{5,475},{6,264},{7,329},{8... | collective-permute-start | bytes 393224 | tf_op jit(solution)/shard_map/ppermute | solution.py:369
  22.2 0.7 copy-start.3
  30.3 35.8 %copy-start.4 = (s32[32]{0:T(128)S(1)}, s32[32]{0:T(128)}, u32[]{:S(2)}) copy-start(s32[32]{0:T(128)} %plan_ref.1) | copy-start | bytes 388
  31.9 25.0 %collective-permute-start.4 = (f32[32,1024]{1,0:T(8,128)S(1)}, f32[32,1024]{1,0:T(8,128)S(1)}, u32[]{:S(2)}, u32[]{:S(2)}) collective-permute-start(f32[32,1024]{1,0:T(8,128)S(1)} %get-tuple-element.15), channel_id=1, source_target_pairs={{0,1},{1,0},{2,3},{3,2},{4,5},{5,4},{6,7},{7,6},{8,9},{9,8},{10,11... | collective-permute-start | bytes 393224 | tf_op jit(solution)/shard_map/ppermute | solution.py:406
  33.8 12.7 %collective-permute-start.5 = (f32[1,128]{1,0:T(1,128)S(1)}, f32[1,128]{1,0:T(1,128)S(1)}, u32[]{:S(2)}, u32[]{:S(2)}) collective-permute-start(f32[1,128]{1,0:T(1,128)S(1)} %get-tuple-element.16.near_ref), channel_id=1, source_target_pairs={{0,270},{1,271},{2,268},{3,269},{4,266},{5,267},{6,264},{7,265},{8... | collective-permute-start | bytes 1544 | tf_op jit(solution)/shard_map/ppermute | solution.py:397
  57.6 20.3 %all-to-all-start.1 = ((f32[8,4,1152]{2,1,0:T(4,128)}), f32[8,4,1152]{2,1,0:T(4,128)S(1)}, u32[]{:S(2)}, u32[]{:S(2)}) async-start(f32[8,4,1152]{2,1,0:T(4,128)} %shard_map.74), calls=%async_computation.1 | async-start | bytes 294912 | tf_op jit(solution)/shard_map/all_to_all | solution.py:408

commit v5 on v4

--- a/solution.py
+++ b/solution.py
@@ -251,13 +251,11 @@
     return step, zh * column + here, zh * column + there, (1 - zh) * column + there
 
 
-def prep_body(occupation_ref, notes_ref):
-    step, *owners = whereabouts()
+def prep_body(notes_ref):
+    step = whereabouts()[0]
     lane = lax.broadcasted_iota(jnp.int32, (1, notes_ref.shape[1]), 1)
-    rows = [jnp.full(lane.shape, occupation_ref[owner * 2 + at]) for owner in owners for at in range(2)]
-    rows += [jnp.where(lane == level, 1.0, 0.0) for level in (step, SIZES[1] * SIZES[2] + step)]
-    for at, row in enumerate(rows):
-        notes_ref[at : at + 1] = row
+    notes_ref[0:1] = jnp.where(lane == step, 1.0, 0.0)
+    notes_ref[1:2] = jnp.where(lane == SIZES[1] * SIZES[2] + step, 1.0, 0.0)
 
 
 def picks_body(plan_ref, picks_ref):
@@ -268,26 +266,28 @@
         picks_ref[slot : slot + 1] = jnp.where(lane == plan_ref[group * slots + slot], 1.0, 0.0)
 
 
-def taken(first_ref, second_ref, first):
-    return jnp.where(first, first_ref[...], second_ref[...])
-
-
-def weights_of(notes_ref, which, own):
-    return [notes_ref[which * own + at : which * own + at + 1, 0:1] for at in range(own)]
-
-
-NEAR, FAR = 1, 2
-
-
-def forward_body(which, low_ref, high_ref, mine_ref, table_ref, kernel_ref, notes_ref, shaped_ref, energy_ref, partner_ref):
+def weights_of(occupation_ref, which, own):
+    owner = whereabouts()[which]
+    return [occupation_ref[owner * own + at] for at in range(own)]
+
+
+MINE, NEAR, FAR = 1, 2, 3
+
+
+def forward_body(which, *refs):
+    halves = 1 if which == FAR else 2
+    occupation_ref, partners = refs[0], refs[1 : 1 + halves]
+    mine_ref, table_ref, kernel_ref, _, shaped_ref, energy_ref, partner_ref = refs[1 + halves :]
     own, points, _ = mine_ref.shape
-    partner = taken(low_ref, high_ref, lax.axis_index("zh") == 0)
+    partner = partners[0][...]
+    if halves == 2:
+        partner = jnp.where(lax.axis_index("zh") == 0, partner, partners[1][...])
     partner_ref[...] = partner
     shaped, energy = forward(
         mine_ref[...],
         partner,
-        weights_of(notes_ref, 0, own),
-        weights_of(notes_ref, which, own),
+        weights_of(occupation_ref, MINE, own),
+        weights_of(occupation_ref, which, own),
         in_mode_order(kernel_ref[...], points),
         unpacked(table_ref, own, points),
     )
@@ -295,12 +295,12 @@
     energy_ref[...] = jnp.full(energy_ref.shape, jnp.sum(energy))
 
 
-def back_body(near_ref, far_ref, table_ref, notes_ref, near_shaped_ref, far_shaped_ref, keep_ref, send_ref):
+def back_body(occupation_ref, near_ref, far_ref, table_ref, near_shaped_ref, far_shaped_ref, keep_ref, send_ref):
     own, points, _ = near_ref.shape
     exchange = backward(
         jnp.concatenate([near_shaped_ref[...], far_shaped_ref[...]], axis=0),
         [near_ref[...], far_ref[...]],
-        [weights_of(notes_ref, which, own) for which in (NEAR, FAR)],
+        [weights_of(occupation_ref, which, own) for which in (NEAR, FAR)],
         unpacked(table_ref, own, points),
     )
     half = exchange.shape[0] // 2
@@ -311,7 +311,7 @@
 
 
 def rows_body(near_ref, across_ref, far_ref, notes_ref, out_ref):
-    row = (near_ref[...] + across_ref[...]) * notes_ref[6:7] + 2.0 * far_ref[...] * notes_ref[7:8]
+    row = (near_ref[...] + across_ref[...]) * notes_ref[0:1] + 2.0 * far_ref[...] * notes_ref[1:2]
     out_ref[...] = jnp.broadcast_to(row[None], out_ref.shape)
 
 
@@ -365,11 +365,12 @@
     slots = plan.shape[0] // groups
     column = lax.axis_size(("y", "x"))
 
-    def moved(move, half):
+    def moved(move, half=None):
         return lax.ppermute(orbitals, AXES, routes(move, half))
 
-    far = [moved(other_half, 1), moved(other_half, 0)]
-    near = [moved(same_half, 0), moved(same_half, 1)]
+    near_low = moved(same_half, 0)
+    far = moved(other_half)
+    near_high = moved(same_half, 1)
 
     table = jnp.asarray(tables(points, own, groups, cores))
     rows = own * points
@@ -388,21 +389,24 @@
             compiler_params=PARAMS,
         )(*arrays)
 
-    notes = call(prep_body, floats(8, 128), occupations, smem=1, flops=1 << 30)
+    notes = call(prep_body, floats(8, 128), flops=1 << 30)
     spectral = (floats(pairs * points, cells), floats(1, 128), jax.ShapeDtypeStruct(orbitals.shape, orbitals.dtype))
     work = 6 * pairs * points * cells * (pairs * points + 384)
+    shared = (orbitals, table, kernel, notes)
     near_shaped, near_energy, near = call(
-        functools.partial(forward_body, NEAR), spectral, *near, orbitals, table, kernel, notes, flops=work
+        functools.partial(forward_body, NEAR), spectral, occupations, near_low, near_high, *shared, smem=1, flops=work
     )
     across = lax.ppermute(near_energy, AXES, routes(mirror))
     picks = call(picks_body, floats(slots, 128), plan, smem=1)
     far_shaped, far_energy, far = call(
-        functools.partial(forward_body, FAR), spectral, *far, orbitals, table, kernel, notes, flops=work
+        functools.partial(forward_body, FAR), spectral, occupations, far, *shared, smem=1, flops=work
     )
     energies = call(rows_body, floats(column * cores, 1, 128), near_energy, across, far_energy, notes)
     everyone = lax.all_to_all(energies, ("y", "x", "core"), 0, 0, tiled=True)
     half = floats(rows // 2, cells)
-    keep, send = call(back_body, (half, half), near, far, table, notes, near_shaped, far_shaped, flops=2 * work)
+    keep, send = call(
+        back_body, (half, half), occupations, near, far, table, near_shaped, far_shaped, smem=1, flops=2 * work
+    )
     received = lax.ppermute(send, AXES, routes(other_core))
     joined = call(join_body, floats(chips, each, cells + 128), keep, received, everyone)
     pieces = lax.all_to_all(joined, "zl", 0, 0, tiled=True)

time: 78.9 us -> 74.5 us (0.944)
  starting transfers between devices: 43.1 us -> 33 us
  waiting for transfers between devices: 17.5 us -> 21.7 us
  blocking collectives: 10.3 us -> 11.4 us
  Pallas kernels: 6.1 us -> 7.18 us
    ppermute x1, starting transfers between devices: 11.2 us -> 5.92 us  [on_device(): across = lax.ppermute(near_energy, AXES, routes(mirror))]
    ppermute x4 -> x3, waiting for transfers between devices: 4.76 us -> 8 us  [moved(): return lax.ppermute(orbitals, AXES, routes(move, half))]
    all_to_all x1, starting transfers between devices: 8.52 us -> 5.97 us  [on_device(): pieces = lax.all_to_all(joined, 'zl', 0, 0, tiled=True)]
    ppermute x4 -> x3, starting transfers between devices: 21.5 us -> 19.2 us  [moved(): return lax.ppermute(orbitals, AXES, routes(move, half))]
    all_to_all x1, blocking collectives: 10.3 us -> 11.4 us  [on_device(): everyone = lax.all_to_all(energies, ('y', 'x', 'core'), 0, 0, tiled=True)]
    pallas_call x8, Pallas kernels: 6.1 us -> 7.18 us  [call(): pl.pallas_call(body, out_shape=out_shape, in_specs=in_smem(smem) + in_vme...]
    ppermute x1, waiting for transfers between devices: 1.53 us -> 2.54 us  [on_device(): across = lax.ppermute(near_energy, AXES, routes(mirror))]
  transfers between devices with their start and end apart: 7 -> 6, of which waited for: 3 -> 3; matrix products, arithmetic and copies ran while one was open for 0% -> 0% of each run, Pallas kernels for 3% -> 3%
where the time goes in v5:
time: 74.5 us; the launch traced here: 74.1 us
  starting transfers between devices  33 us (44%)
  waiting for transfers between devices  21.7 us (29%)
  blocking collectives  11.4 us (15%)
  Pallas kernels  7.18 us (10%)
  between operations  0.78 us (1%)
    ppermute x3, starting transfers between devices, moved(): return lax.ppermute(orbitals, AXES, routes(move, half))  19.2 us
    all_to_all x1, blocking collectives, on_device(): everyone = lax.all_to_all(energies, ('y', 'x', 'core'), 0, 0, tiled=True)  11.4 us
    all_to_all x1, waiting for transfers between devices, on_device(): pieces = lax.all_to_all(joined, 'zl', 0, 0, tiled=True)  11.2 us
    ppermute x3, waiting for transfers between devices, moved(): return lax.ppermute(orbitals, AXES, routes(move, half))  8 us
    pallas_call x8, Pallas kernels, call(): pl.pallas_call(body, out_shape=out_shape, in_specs=in_smem(smem) + in_vme...  7.18 us
    all_to_all x1, starting transfers between devices, on_device(): pieces = lax.all_to_all(joined, 'zl', 0, 0, tiled=True)  5.97 us
    ppermute x1, starting transfers between devices, on_device(): across = lax.ppermute(near_energy, AXES, routes(mirror))  5.92 us
    ppermute x1, waiting for transfers between devices, on_device(): across = lax.ppermute(near_energy, AXES, routes(mirror))  2.54 us
  transfers between devices with their start and end apart: 6, of which 3 were waited for; matrix products, arithmetic and copies ran while one was open for 0% of the time, Pallas kernels for 3%

profile of v5, /device:TPU:32, one launch (start us, length us, event | category | flops | bytes accessed | tf_op | source)
XLA Modules:
  0.0 74.1 jit_solution(14932012875701931544)
XLA Ops:
  0.6 0.0 copy-start
  0.6 0.0 copy-start.1
  0.7 0.0 copy-start.2
  0.7 16.3 %collective-permute-start.2 = (bf16[2,32,1024]{2,1,0:T(8,128)(2,1)}, bf16[2,32,1024]{2,1,0:T(8,128)(2,1)S(1)}, u32[]{:S(2)}, u32[]{:S(2)}) collective-permute-start(bf16[2,32,1024]{2,1,0:T(8,128)(2,1)} %refs_2_.1), channel_id=1, source_target_pairs={{0,430},{1,415},{2,444},{3,493},{4,506},{5,475},{6,264},{7,329},{8... | collective-permute-start | bytes 393224 | tf_op jit(solution)/shard_map/ppermute | solution.py:369
  17.0 2.2 %collective-permute-start = (bf16[2,32,1024]{2,1,0:T(8,128)(2,1)}, bf16[2,32,1024]{2,1,0:T(8,128)(2,1)S(1)}, u32[]{:S(2)}, u32[]{:S(2)}) collective-permute-start(bf16[2,32,1024]{2,1,0:T(8,128)(2,1)} %refs_2_.1), channel_id=1, source_target_pairs={{0,160},{1,145},{2,178},{3,227},{4,244},{5,213},{6,6},{7,71},{8,24... | collective-permute-start | bytes 393224 | tf_op jit(solution)/shard_map/ppermute | solution.py:369
  19.2 0.7 collective-permute-start.1
  19.9 8.0 %collective-permute-done.2.refs_1_ = bf16[2,32,1024]{2,1,0:T(8,128)(2,1)S(1)} collective-permute-done((bf16[2,32,1024]{2,1,0:T(8,128)(2,1)}, bf16[2,32,1024]{2,1,0:T(8,128)(2,1)S(1)}, u32[]{:S(2)}, u32[]{:S(2)}) %collective-permute-start.2) | collective-permute-done | bytes 131104 | tf_op jit(solution)/shard_map/ppermute | solution.py:369
  27.9 0.0 copy-done.1
  27.9 1.6 %shard_map.71 = (f32[128,1024]{1,0:T(8,128)S(1)}, f32[1,128]{1,0:T(1,128)S(1)}, bf16[2,32,1024]{2,1,0:T(8,128)(2,1)S(1)}) custom-call(f32[64]{0:T(128)S(1)} %copy-done.3, bf16[2,32,1024]{2,1,0:T(8,128)(2,1)S(1)} %collective-permute-done.2.refs_1_, bf16[2,32,1024]{2,1,0:T(8,128)(2,1)S(1)} %copy-done.1, bf16[3456,256]{1,0:T(8,128)(2,1)S(1)} %copy-done, ...), custom_call_target="tpu_custom_call" | custom-call | flops 402653184 | bytes 1048576 | tf_op jit(solution)/shard_map/pallas_call | solution.py:383
  29.5 0.0 collective-permute-done.refs_1_
  29.5 0.0 collective-permute-done.1.refs_2_
  29.5 1.6 %shard_map.70 = (f32[128,1024]{1,0:T(8,128)S(1)}, f32[1,128]{1,0:T(1,128)S(1)}, bf16[2,32,1024]{2,1,0:T(8,128)(2,1)S(1)}) custom-call(f32[64]{0:T(128)S(1)} %copy-done.3, bf16[2,32,1024]{2,1,0:T(8,128)(2,1)S(1)} %collective-permute-done.refs_1_, bf16[2,32,1024]{2,1,0:T(8,128)(2,1)S(1)} %collective-permute-done.1.refs_2_, bf16[2,32,1024]{2,1,0:T(8,128)(2,1)S(1)} %copy-done.1, ...), custom_call_target="tpu_custom_call" | custom-call | flops 402653184 | bytes 1048576 | tf_op jit(solution)/shard_map/pallas_call | solution.py:383
  31.1 0.0 copy-start.4
  31.2 2.0 %shard_map.72 = (f32[32,1024]{1,0:T(8,128)S(1)}, f32[32,1024]{1,0:T(8,128)S(1)}) custom-call(f32[64]{0:T(128)S(1)} %copy-done.3, bf16[2,32,1024]{2,1,0:T(8,128)(2,1)S(1)} %get-tuple-element.10.near_ref, bf16[2,32,1024]{2,1,0:T(8,128)(2,1)S(1)} %get-tuple-element.11.far_ref, bf16[3456,256]{1,0:T(8,128)(2,1)S(1)} %copy-done, ...), custom_call_target="tpu_custom_call" | custom-call | flops 805306368 | bytes 1048576 | tf_op jit(solution)/shard_map/pallas_call | solution.py:383
  33.2 1.9 %collective-permute-start.3 = (f32[32,1024]{1,0:T(8,128)S(1)}, f32[32,1024]{1,0:T(8,128)S(1)}, u32[]{:S(2)}, u32[]{:S(2)}) collective-permute-start(f32[32,1024]{1,0:T(8,128)S(1)} %get-tuple-element.15), channel_id=1, source_target_pairs={{0,1},{1,0},{2,3},{3,2},{4,5},{5,4},{6,7},{7,6},{8,9},{9,8},{10,11... | collective-permute-start | bytes 393224 | tf_op jit(solution)/shard_map/ppermute | solution.py:410
  35.1 5.9 %collective-permute-start.4 = (f32[1,128]{1,0:T(1,128)S(1)}, f32[1,128]{1,0:T(1,128)S(1)}, u32[]{:S(2)}, u32[]{:S(2)}) collective-permute-start(f32[1,128]{1,0:T(1,128)S(1)} %get-tuple-element.16.near_ref), channel_id=1, source_target_pairs={{0,270},{1,271},{2,268},{3,269},{4,266},{5,267},{6,264},{7,265},{8... | collective-permute-start | bytes 1544 | tf_op jit(solution)/shard_map/ppermute | solution.py:399
  41.1 2.5 %collective-permute-done.4.across_ref = f32[1,128]{1,0:T(1,128)S(1)} collective-permute-done((f32[1,128]{1,0:T(1,128)S(1)}, f32[1,128]{1,0:T(1,128)S(1)}, u32[]{:S(2)}, u32[]{:S(2)}) %collective-permute-start.4) | collective-permute-done | bytes 544 | tf_op jit(solution)/shard_map/ppermute | solution.py:399
  43.6 11.4 %all_to_all.10.energies_ref = f32[32,1,128]{2,1,0:T(1,128)S(1)} all-to-all(f32[32,1,128]{2,1,0:T(1,128)S(1)} %shard_map.73), channel_id=1, replica_groups=mesh['zh'=2,'y'=4,'x'=4,'zl'=8,'core'=2] {'y','x','core'}, dimensions={0} | all-to-all | bytes 32768 | tf_op jit(solution)/shard_map/all_to_all | solution.py:405
  55.0 0.0 collective-permute-done.3.received_ref
  55.1 0.7 shard_map.74
  55.8 6.0 %all-to-all-start.1 = ((f32[8,4,1152]{2,1,0:T(4,128)}), f32[8,4,1152]{2,1,0:T(4,128)S(1)}, u32[]{:S(2)}, u32[]{:S(2)}) async-start(f32[8,4,1152]{2,1,0:T(4,128)} %shard_map.74), calls=%async_computation.1 | async-start | bytes 294912 | tf_op jit(solution)/shard_map/all_to_all | solution.py:412
  61.7 0.6 shard_map.68.picks_ref
  62.3 11.2 %all-to-all-done.1.pieces_ref = f32[8,4,1152]{2,1,0:T(4,128)S(1)} async-done(((f32[8,4,1152]{2,1,0:T(4,128)}), f32[8,4,1152]{2,1,0:T(4,128)S(1)}, u32[]{:S(2)}, u32[]{:S(2)}) %all-to-all-start.1) | async-done | bytes 147488 | tf_op jit(solution)/shard_map/all_to_all | solution.py:412
  73.5 0.6 shard_map.75
  (7 shorter events, 0.1 us)
Async XLA Ops:
  0.6 27.3 %copy-start = (bf16[3456,256]{1,0:T(8,128)(2,1)S(1)}, bf16[3456,256]{1,0:T(8,128)(2,1)}, u32[]{:S(2)}) copy-start(bf16[3456,256]{1,0:T(8,128)(2,1)} %constant.2.clone.refs_4_.refs_3_.table_ref) | copy-start | bytes 5308420
  0.6 27.3 %copy-start.1 = (bf16[2,32,1024]{2,1,0:T(8,128)(2,1)S(1)}, bf16[2,32,1024]{2,1,0:T(8,128)(2,1)}, u32[]{:S(2)}) copy-start(bf16[2,32,1024]{2,1,0:T(8,128)(2,1)} %refs_2_.1) | copy-start | bytes 393220
  0.7 27.3 %copy-start.2 = (f32[32,1024]{1,0:T(8,128)S(1)}, f32[32,1024]{1,0:T(8,128)}, u32[]{:S(2)}) copy-start(f32[32,1024]{1,0:T(8,128)} %refs_4_.2) | copy-start | bytes 393220
  0.7 27.2 %copy-start.3 = (f32[64]{0:T(128)S(1)}, f32[64]{0:T(128)}, u32[]{:S(2)}) copy-start(f32[64]{0:T(128)} %occupation_ref.1) | copy-start | bytes 772
  0.7 27.2 %collective-permute-start.2 = (bf16[2,32,1024]{2,1,0:T(8,128)(2,1)}, bf16[2,32,1024]{2,1,0:T(8,128)(2,1)S(1)}, u32[]{:S(2)}, u32[]{:S(2)}) collective-permute-start(bf16[2,32,1024]{2,1,0:T(8,128)(2,1)} %refs_2_.1), channel_id=1, source_target_pairs={{0,430},{1,415},{2,444},{3,493},{4,506},{5,475},{6,264},{7,329},{8... | collective-permute-start | bytes 393224 | tf_op jit(solution)/shard_map/ppermute | solution.py:369
  17.0 12.5 %collective-permute-start = (bf16[2,32,1024]{2,1,0:T(8,128)(2,1)}, bf16[2,32,1024]{2,1,0:T(8,128)(2,1)S(1)}, u32[]{:S(2)}, u32[]{:S(2)}) collective-permute-start(bf16[2,32,1024]{2,1,0:T(8,128)(2,1)} %refs_2_.1), channel_id=1, source_target_pairs={{0,160},{1,145},{2,178},{3,227},{4,244},{5,213},{6,6},{7,71},{8,24... | collective-permute-start | bytes 393224 | tf_op jit(solution)/shard_map/ppermute | solution.py:369
  19.2 10.3 %collective-permute-start.1 = (bf16[2,32,1024]{2,1,0:T(8,128)(2,1)}, bf16[2,32,1024]{2,1,0:T(8,128)(2,1)S(1)}, u32[]{:S(2)}, u32[]{:S(2)}) collective-permute-start(bf16[2,32,1024]{2,1,0:T(8,128)(2,1)} %refs_2_.1), channel_id=1, source_target_pairs={{256,352},{257,385},{258,290},{259,451},{260,372},{261,341},{262,2... | collective-permute-start | bytes 393224 | tf_op jit(solution)/shard_map/ppermute | solution.py:369
  31.1 30.6 %copy-start.4 = (s32[32]{0:T(128)S(1)}, s32[32]{0:T(128)}, u32[]{:S(2)}) copy-start(s32[32]{0:T(128)} %plan_ref.1) | copy-start | bytes 388
  33.2 21.8 %collective-permute-start.3 = (f32[32,1024]{1,0:T(8,128)S(1)}, f32[32,1024]{1,0:T(8,128)S(1)}, u32[]{:S(2)}, u32[]{:S(2)}) collective-permute-start(f32[32,1024]{1,0:T(8,128)S(1)} %get-tuple-element.15), channel_id=1, source_target_pairs={{0,1},{1,0},{2,3},{3,2},{4,5},{5,4},{6,7},{7,6},{8,9},{9,8},{10,11... | collective-permute-start | bytes 393224 | tf_op jit(solution)/shard_map/ppermute | solution.py:410
  35.1 8.5 %collective-permute-start.4 = (f32[1,128]{1,0:T(1,128)S(1)}, f32[1,128]{1,0:T(1,128)S(1)}, u32[]{:S(2)}, u32[]{:S(2)}) collective-permute-start(f32[1,128]{1,0:T(1,128)S(1)} %get-tuple-element.16.near_ref), channel_id=1, source_target_pairs={{0,270},{1,271},{2,268},{3,269},{4,266},{5,267},{6,264},{7,265},{8... | collective-permute-start | bytes 1544 | tf_op jit(solution)/shard_map/ppermute | solution.py:399
  55.8 17.7 %all-to-all-start.1 = ((f32[8,4,1152]{2,1,0:T(4,128)}), f32[8,4,1152]{2,1,0:T(4,128)S(1)}, u32[]{:S(2)}, u32[]{:S(2)}) async-start(f32[8,4,1152]{2,1,0:T(4,128)} %shard_map.74), calls=%async_computation.1 | async-start | bytes 294912 | tf_op jit(solution)/shard_map/all_to_all | solution.py:412

commit v6 on v4

--- a/solution.py
+++ b/solution.py
@@ -268,8 +268,8 @@
         picks_ref[slot : slot + 1] = jnp.where(lane == plan_ref[group * slots + slot], 1.0, 0.0)
 
 
-def taken(first_ref, second_ref, first):
-    return jnp.where(first, first_ref[...], second_ref[...])
+def mine_of(low_ref, high_ref):
+    return jnp.where(lax.axis_index("zh") == 0, low_ref[...], high_ref[...])
 
 
 def weights_of(notes_ref, which, own):
@@ -279,27 +279,32 @@
 NEAR, FAR = 1, 2
 
 
-def forward_body(which, low_ref, high_ref, mine_ref, table_ref, kernel_ref, notes_ref, shaped_ref, energy_ref, partner_ref):
+def forward_body(which, half, partner_ref, mine_ref, table_ref, kernel_ref, notes_ref, shaped_ref, energy_ref):
     own, points, _ = mine_ref.shape
-    partner = taken(low_ref, high_ref, lax.axis_index("zh") == 0)
-    partner_ref[...] = partner
-    shaped, energy = forward(
-        mine_ref[...],
-        partner,
-        weights_of(notes_ref, 0, own),
-        weights_of(notes_ref, which, own),
-        in_mode_order(kernel_ref[...], points),
-        unpacked(table_ref, own, points),
-    )
-    shaped_ref[...] = shaped
-    energy_ref[...] = jnp.full(energy_ref.shape, jnp.sum(energy))
-
-
-def back_body(near_ref, far_ref, table_ref, notes_ref, near_shaped_ref, far_shaped_ref, keep_ref, send_ref):
-    own, points, _ = near_ref.shape
+
+    def run():
+        shaped, energy = forward(
+            mine_ref[...],
+            partner_ref[...],
+            weights_of(notes_ref, 0, own),
+            weights_of(notes_ref, which, own),
+            in_mode_order(kernel_ref[...], points),
+            unpacked(table_ref, own, points),
+        )
+        shaped_ref[...] = shaped
+        energy_ref[...] = jnp.full(energy_ref.shape, jnp.sum(energy))
+
+    if half is None:
+        run()
+    else:
+        pl.when(lax.axis_index("zh") == half)(run)
+
+
+def back_body(low_ref, high_ref, far_ref, table_ref, notes_ref, low_shaped_ref, high_shaped_ref, far_shaped_ref, keep_ref, send_ref):
+    own, points, _ = far_ref.shape
     exchange = backward(
-        jnp.concatenate([near_shaped_ref[...], far_shaped_ref[...]], axis=0),
-        [near_ref[...], far_ref[...]],
+        jnp.concatenate([mine_of(low_shaped_ref, high_shaped_ref), far_shaped_ref[...]], axis=0),
+        [mine_of(low_ref, high_ref), far_ref[...]],
         [weights_of(notes_ref, which, own) for which in (NEAR, FAR)],
         unpacked(table_ref, own, points),
     )
@@ -310,8 +315,9 @@
     send_ref[...] = jnp.where(core == 0, high, low)
 
 
-def rows_body(near_ref, across_ref, far_ref, notes_ref, out_ref):
-    row = (near_ref[...] + across_ref[...]) * notes_ref[6:7] + 2.0 * far_ref[...] * notes_ref[7:8]
+def rows_body(low_ref, high_ref, down_ref, up_ref, far_ref, notes_ref, out_ref):
+    near = mine_of(low_ref, high_ref) + mine_of(down_ref, up_ref)
+    row = near * notes_ref[6:7] + 2.0 * far_ref[...] * notes_ref[7:8]
     out_ref[...] = jnp.broadcast_to(row[None], out_ref.shape)
 
 
@@ -365,11 +371,12 @@
     slots = plan.shape[0] // groups
     column = lax.axis_size(("y", "x"))
 
-    def moved(move, half):
-        return lax.ppermute(orbitals, AXES, routes(move, half))
-
-    far = [moved(other_half, 1), moved(other_half, 0)]
-    near = [moved(same_half, 0), moved(same_half, 1)]
+    def moved(value, move, half=None):
+        return lax.ppermute(value, AXES, routes(move, half))
+
+    near_low = moved(orbitals, same_half, 0)
+    far = moved(orbitals, other_half)
+    near_high = moved(orbitals, same_half, 1)
 
     table = jnp.asarray(tables(points, own, groups, cores))
     rows = own * points
@@ -389,20 +396,25 @@
         )(*arrays)
 
     notes = call(prep_body, floats(8, 128), occupations, smem=1, flops=1 << 30)
-    spectral = (floats(pairs * points, cells), floats(1, 128), jax.ShapeDtypeStruct(orbitals.shape, orbitals.dtype))
+    spectral = (floats(pairs * points, cells), floats(1, 128))
     work = 6 * pairs * points * cells * (pairs * points + 384)
-    near_shaped, near_energy, near = call(
-        functools.partial(forward_body, NEAR), spectral, *near, orbitals, table, kernel, notes, flops=work
-    )
-    across = lax.ppermute(near_energy, AXES, routes(mirror))
+    shared = (orbitals, table, kernel, notes)
+
+    def forwards(which, half, partner):
+        body = functools.partial(forward_body, which, half)
+        return call(body, spectral, partner, *shared, flops=work)
+
+    low_shaped, low_energy = forwards(NEAR, 0, near_low)
+    up = moved(low_energy, mirror, 0)
+    high_shaped, high_energy = forwards(NEAR, 1, near_high)
+    down = moved(high_energy, mirror, 1)
     picks = call(picks_body, floats(slots, 128), plan, smem=1)
-    far_shaped, far_energy, far = call(
-        functools.partial(forward_body, FAR), spectral, *far, orbitals, table, kernel, notes, flops=work
-    )
-    energies = call(rows_body, floats(column * cores, 1, 128), near_energy, across, far_energy, notes)
+    far_shaped, far_energy = forwards(FAR, None, far)
+    energies = call(rows_body, floats(column * cores, 1, 128), low_energy, high_energy, down, up, far_energy, notes)
     everyone = lax.all_to_all(energies, ("y", "x", "core"), 0, 0, tiled=True)
     half = floats(rows // 2, cells)
-    keep, send = call(back_body, (half, half), near, far, table, notes, near_shaped, far_shaped, flops=2 * work)
+    shaped = (low_shaped, high_shaped, far_shaped)
+    keep, send = call(back_body, (half, half), near_low, near_high, far, table, notes, *shaped, flops=2 * work)
     received = lax.ppermute(send, AXES, routes(other_core))
     joined = call(join_body, floats(chips, each, cells + 128), keep, received, everyone)
     pieces = lax.all_to_all(joined, "zl", 0, 0, tiled=True)

time: 78.9 us -> 77.8 us (0.986)
  starting transfers between devices: 43.1 us -> 39.4 us
  waiting for transfers between devices: 17.5 us -> 20.1 us
    ppermute x5, starting transfers between devices: 32.7 us -> 29.7 us  [moved(): return lax.ppermute(value, AXES, routes(move, half))]
    ppermute x5, waiting for transfers between devices: 6.3 us -> 8.93 us  [moved(): return lax.ppermute(value, AXES, routes(move, half))]
    all_to_all x1, starting transfers between devices: 8.52 us -> 7.71 us  [on_device(): pieces = lax.all_to_all(joined, 'zl', 0, 0, tiled=True)]
    pallas_call x8 -> x9, Pallas kernels: 6.1 us -> 6.1 us  [call(): pl.pallas_call(body, out_shape=out_shape, in_specs=in_smem(smem) + in_vme...]
where the time goes in v6:
time: 77.8 us; the launch traced here: 77.4 us
  starting transfers between devices  39.4 us (51%)
  waiting for transfers between devices  20.1 us (26%)
  blocking collectives  10.3 us (13%)
  Pallas kernels  6.1 us (8%)
  between operations  0.82 us (1%)
    ppermute x5, starting transfers between devices, moved(): return lax.ppermute(value, AXES, routes(move, half))  29.7 us
    all_to_all x1, waiting for transfers between devices, on_device(): pieces = lax.all_to_all(joined, 'zl', 0, 0, tiled=True)  11.2 us
    all_to_all x1, blocking collectives, on_device(): everyone = lax.all_to_all(energies, ('y', 'x', 'core'), 0, 0, tiled=True)  10.3 us
    ppermute x5, waiting for transfers between devices, moved(): return lax.ppermute(value, AXES, routes(move, half))  8.93 us
    all_to_all x1, starting transfers between devices, on_device(): pieces = lax.all_to_all(joined, 'zl', 0, 0, tiled=True)  7.71 us
    pallas_call x9, Pallas kernels, call(): pl.pallas_call(body, out_shape=out_shape, in_specs=in_smem(smem) + in_vme...  6.1 us
    ppermute x1, starting transfers between devices, on_device(): received = lax.ppermute(send, AXES, routes(other_core))  1.92 us
  transfers between devices with their start and end apart: 7, of which 3 were waited for; matrix products, arithmetic and copies ran while one was open for 0% of the time, Pallas kernels for 3%

profile of v6, /device:TPU:32, one launch (start us, length us, event | category | flops | bytes accessed | tf_op | source)
XLA Modules:
  0.0 77.4 jit_solution(3156893374005398189)
XLA Ops:
  0.6 0.0 copy-start
  0.7 7.4 %collective-permute-start = (bf16[2,32,1024]{2,1,0:T(8,128)(2,1)}, bf16[2,32,1024]{2,1,0:T(8,128)(2,1)S(1)}, u32[]{:S(2)}, u32[]{:S(2)}) collective-permute-start(bf16[2,32,1024]{2,1,0:T(8,128)(2,1)} %mine_ref.5), channel_id=1, source_target_pairs={{0,160},{1,145},{2,178},{3,227},{4,244},{5,213},{6,6},{7,71},{8,24... | collective-permute-start | bytes 393224 | tf_op jit(solution)/shard_map/ppermute | solution.py:375
  8.1 0.7 collective-permute-start.1
  8.8 11.1 %collective-permute-start.2 = (bf16[2,32,1024]{2,1,0:T(8,128)(2,1)}, bf16[2,32,1024]{2,1,0:T(8,128)(2,1)S(1)}, u32[]{:S(2)}, u32[]{:S(2)}) collective-permute-start(bf16[2,32,1024]{2,1,0:T(8,128)(2,1)} %mine_ref.5), channel_id=1, source_target_pairs={{0,430},{1,415},{2,444},{3,493},{4,506},{5,475},{6,264},{7,329},{8... | collective-permute-start | bytes 393224 | tf_op jit(solution)/shard_map/ppermute | solution.py:375
  19.9 0.6 copy-done.3
  20.5 0.6 shard_map.69.notes_ref
  21.1 0.0 collective-permute-done.partner_ref.low_ref
  21.1 1.1 %shard_map.70 = (f32[128,1024]{1,0:T(8,128)S(1)}, f32[1,128]{1,0:T(1,128)S(1)}) custom-call(bf16[2,32,1024]{2,1,0:T(8,128)(2,1)S(1)} %collective-permute-done.partner_ref.low_ref, bf16[2,32,1024]{2,1,0:T(8,128)(2,1)S(1)} %copy-done.1, bf16[3456,256]{1,0:T(8,128)(2,1)S(1)} %copy-done, f32[32,1024]{1,0:T(8,128)S(1)} %copy-done.2, f32[8,128]{1,0:T(8,128)S(1)} %shard_map.69.notes_ref), custom_call_target="tpu_custom_call" | custom-call | flops 402653184 | bytes 1048576 | tf_op jit(solution)/shard_map/pallas_call | solution.py:389
  22.2 0.0 collective-permute-done.1.partner_ref.high_ref
  22.2 7.7 %collective-permute-done.2.partner_ref.far_ref = bf16[2,32,1024]{2,1,0:T(8,128)(2,1)S(1)} collective-permute-done((bf16[2,32,1024]{2,1,0:T(8,128)(2,1)}, bf16[2,32,1024]{2,1,0:T(8,128)(2,1)S(1)}, u32[]{:S(2)}, u32[]{:S(2)}) %collective-permute-start.2) | collective-permute-done | bytes 131104 | tf_op jit(solution)/shard_map/ppermute | solution.py:375
  29.9 1.0 %shard_map.72 = (f32[128,1024]{1,0:T(8,128)S(1)}, f32[1,128]{1,0:T(1,128)S(1)}) custom-call(bf16[2,32,1024]{2,1,0:T(8,128)(2,1)S(1)} %collective-permute-done.2.partner_ref.far_ref, bf16[2,32,1024]{2,1,0:T(8,128)(2,1)S(1)} %copy-done.1, bf16[3456,256]{1,0:T(8,128)(2,1)S(1)} %copy-done, f32[32,1024]{1,0:T(8,128)S(1)} %copy-done.2, ...), custom_call_target="tpu_custom_call" | custom-call | flops 402653184 | bytes 1048576 | tf_op jit(solution)/shard_map/pallas_call | solution.py:389
  31.0 0.0 copy-start.4
  31.0 1.5 %shard_map.73 = (f32[32,1024]{1,0:T(8,128)S(1)}, f32[32,1024]{1,0:T(8,128)S(1)}) custom-call(bf16[2,32,1024]{2,1,0:T(8,128)(2,1)S(1)} %collective-permute-done.partner_ref.low_ref, bf16[2,32,1024]{2,1,0:T(8,128)(2,1)S(1)} %collective-permute-done.1.partner_ref.high_ref, bf16[2,32,1024]{2,1,0:T(8,128)(2,1)S(1)} %collective-permute-done.2.partner_ref.far_ref, ...), custom_call_target="tpu_custom_call" | custom-call | flops 805306368 | bytes 1048576 | tf_op jit(solution)/shard_map/pallas_call | solution.py:389
  32.5 1.9 %collective-permute-start.3 = (f32[32,1024]{1,0:T(8,128)S(1)}, f32[32,1024]{1,0:T(8,128)S(1)}, u32[]{:S(2)}, u32[]{:S(2)}) collective-permute-start(f32[32,1024]{1,0:T(8,128)S(1)} %get-tuple-element.14), channel_id=1, source_target_pairs={{0,1},{1,0},{2,3},{3,2},{4,5},{5,4},{6,7},{7,6},{8,9},{9,8},{10,11... | collective-permute-start | bytes 393224 | tf_op jit(solution)/shard_map/ppermute | solution.py:418
  34.4 1.3 %collective-permute-start.4 = (f32[1,128]{1,0:T(1,128)S(1)}, f32[1,128]{1,0:T(1,128)S(1)}, u32[]{:S(2)}, u32[]{:S(2)}) collective-permute-start(f32[1,128]{1,0:T(1,128)S(1)} %get-tuple-element.16.high_ref), channel_id=1, source_target_pairs={{256,14},{257,15},{258,12},{259,13},{260,10},{261,11},{262,8},{263... | collective-permute-start | bytes 1544 | tf_op jit(solution)/shard_map/ppermute | solution.py:375
  35.7 9.3 %collective-permute-start.5 = (f32[1,128]{1,0:T(1,128)S(1)}, f32[1,128]{1,0:T(1,128)S(1)}, u32[]{:S(2)}, u32[]{:S(2)}) collective-permute-start(f32[1,128]{1,0:T(1,128)S(1)} %get-tuple-element.15.low_ref), channel_id=1, source_target_pairs={{0,270},{1,271},{2,268},{3,269},{4,266},{5,267},{6,264},{7,265},{8... | collective-permute-start | bytes 1544 | tf_op jit(solution)/shard_map/ppermute | solution.py:375
  45.0 0.0 collective-permute-done.4.down_ref
  45.0 1.3 %collective-permute-done.5.up_ref = f32[1,128]{1,0:T(1,128)S(1)} collective-permute-done((f32[1,128]{1,0:T(1,128)S(1)}, f32[1,128]{1,0:T(1,128)S(1)}, u32[]{:S(2)}, u32[]{:S(2)}) %collective-permute-start.5) | collective-permute-done | bytes 544 | tf_op jit(solution)/shard_map/ppermute | solution.py:375
  46.3 10.3 %all_to_all.10.energies_ref = f32[32,1,128]{2,1,0:T(1,128)S(1)} all-to-all(f32[32,1,128]{2,1,0:T(1,128)S(1)} %shard_map.74), channel_id=1, replica_groups=mesh['zh'=2,'y'=4,'x'=4,'zl'=8,'core'=2] {'y','x','core'}, dimensions={0} | all-to-all | bytes 32768 | tf_op jit(solution)/shard_map/all_to_all | solution.py:414
  56.6 0.7 shard_map.75
  57.3 7.7 %all-to-all-start.1 = ((f32[8,4,1152]{2,1,0:T(4,128)}), f32[8,4,1152]{2,1,0:T(4,128)S(1)}, u32[]{:S(2)}, u32[]{:S(2)}) async-start(f32[8,4,1152]{2,1,0:T(4,128)} %shard_map.75), calls=%async_computation.1 | async-start | bytes 294912 | tf_op jit(solution)/shard_map/all_to_all | solution.py:420
  65.0 0.6 shard_map.68.picks_ref
  65.6 11.2 %all-to-all-done.1.pieces_ref = f32[8,4,1152]{2,1,0:T(4,128)S(1)} async-done(((f32[8,4,1152]{2,1,0:T(4,128)}), f32[8,4,1152]{2,1,0:T(4,128)S(1)}, u32[]{:S(2)}, u32[]{:S(2)}) %all-to-all-start.1) | async-done | bytes 147488 | tf_op jit(solution)/shard_map/all_to_all | solution.py:420
  76.8 0.6 shard_map.76
  (10 shorter events, 0.1 us)
Async XLA Ops:
  0.6 20.5 %copy-start = (bf16[3456,256]{1,0:T(8,128)(2,1)S(1)}, bf16[3456,256]{1,0:T(8,128)(2,1)}, u32[]{:S(2)}) copy-start(bf16[3456,256]{1,0:T(8,128)(2,1)} %constant.2.clone.table_ref) | copy-start | bytes 5308420
  0.6 20.5 %copy-start.1 = (bf16[2,32,1024]{2,1,0:T(8,128)(2,1)S(1)}, bf16[2,32,1024]{2,1,0:T(8,128)(2,1)}, u32[]{:S(2)}) copy-start(bf16[2,32,1024]{2,1,0:T(8,128)(2,1)} %mine_ref.5) | copy-start | bytes 393220
  0.7 20.5 %copy-start.2 = (f32[32,1024]{1,0:T(8,128)S(1)}, f32[32,1024]{1,0:T(8,128)}, u32[]{:S(2)}) copy-start(f32[32,1024]{1,0:T(8,128)} %kernel_ref.5) | copy-start | bytes 393220
  0.7 20.4 %collective-permute-start = (bf16[2,32,1024]{2,1,0:T(8,128)(2,1)}, bf16[2,32,1024]{2,1,0:T(8,128)(2,1)S(1)}, u32[]{:S(2)}, u32[]{:S(2)}) collective-permute-start(bf16[2,32,1024]{2,1,0:T(8,128)(2,1)} %mine_ref.5), channel_id=1, source_target_pairs={{0,160},{1,145},{2,178},{3,227},{4,244},{5,213},{6,6},{7,71},{8,24... | collective-permute-start | bytes 393224 | tf_op jit(solution)/shard_map/ppermute | solution.py:375
  8.1 14.1 %collective-permute-start.1 = (bf16[2,32,1024]{2,1,0:T(8,128)(2,1)}, bf16[2,32,1024]{2,1,0:T(8,128)(2,1)S(1)}, u32[]{:S(2)}, u32[]{:S(2)}) collective-permute-start(bf16[2,32,1024]{2,1,0:T(8,128)(2,1)} %mine_ref.5), channel_id=1, source_target_pairs={{256,352},{257,385},{258,290},{259,451},{260,372},{261,341},{262,2... | collective-permute-start | bytes 393224 | tf_op jit(solution)/shard_map/ppermute | solution.py:375
  8.8 21.1 %collective-permute-start.2 = (bf16[2,32,1024]{2,1,0:T(8,128)(2,1)}, bf16[2,32,1024]{2,1,0:T(8,128)(2,1)S(1)}, u32[]{:S(2)}, u32[]{:S(2)}) collective-permute-start(bf16[2,32,1024]{2,1,0:T(8,128)(2,1)} %mine_ref.5), channel_id=1, source_target_pairs={{0,430},{1,415},{2,444},{3,493},{4,506},{5,475},{6,264},{7,329},{8... | collective-permute-start | bytes 393224 | tf_op jit(solution)/shard_map/ppermute | solution.py:375
  19.9 0.7 copy-start.3
  31.0 34.1 %copy-start.4 = (s32[32]{0:T(128)S(1)}, s32[32]{0:T(128)}, u32[]{:S(2)}) copy-start(s32[32]{0:T(128)} %plan_ref.1) | copy-start | bytes 388
  32.5 24.2 %collective-permute-start.3 = (f32[32,1024]{1,0:T(8,128)S(1)}, f32[32,1024]{1,0:T(8,128)S(1)}, u32[]{:S(2)}, u32[]{:S(2)}) collective-permute-start(f32[32,1024]{1,0:T(8,128)S(1)} %get-tuple-element.14), channel_id=1, source_target_pairs={{0,1},{1,0},{2,3},{3,2},{4,5},{5,4},{6,7},{7,6},{8,9},{9,8},{10,11... | collective-permute-start | bytes 393224 | tf_op jit(solution)/shard_map/ppermute | solution.py:418
  34.4 10.6 %collective-permute-start.4 = (f32[1,128]{1,0:T(1,128)S(1)}, f32[1,128]{1,0:T(1,128)S(1)}, u32[]{:S(2)}, u32[]{:S(2)}) collective-permute-start(f32[1,128]{1,0:T(1,128)S(1)} %get-tuple-element.16.high_ref), channel_id=1, source_target_pairs={{256,14},{257,15},{258,12},{259,13},{260,10},{261,11},{262,8},{263... | collective-permute-start | bytes 1544 | tf_op jit(solution)/shard_map/ppermute | solution.py:375
  35.7 10.6 %collective-permute-start.5 = (f32[1,128]{1,0:T(1,128)S(1)}, f32[1,128]{1,0:T(1,128)S(1)}, u32[]{:S(2)}, u32[]{:S(2)}) collective-permute-start(f32[1,128]{1,0:T(1,128)S(1)} %get-tuple-element.15.low_ref), channel_id=1, source_target_pairs={{0,270},{1,271},{2,268},{3,269},{4,266},{5,267},{6,264},{7,265},{8... | collective-permute-start | bytes 1544 | tf_op jit(solution)/shard_map/ppermute | solution.py:375
  57.3 19.5 %all-to-all-start.1 = ((f32[8,4,1152]{2,1,0:T(4,128)}), f32[8,4,1152]{2,1,0:T(4,128)S(1)}, u32[]{:S(2)}, u32[]{:S(2)}) async-start(f32[8,4,1152]{2,1,0:T(4,128)} %shard_map.75), calls=%async_computation.1 | async-start | bytes 294912 | tf_op jit(solution)/shard_map/all_to_all | solution.py:420

commit v7 on v3

--- a/solution.py
+++ b/solution.py
@@ -22,8 +22,8 @@
     ((3, 3), (3, 1)),
     ((0, 0), (1, 0)),
     ((0, 1), (0, 3)),
-    ((1, 3), (1, 1)),
-    ((0, 2), (3, 0)),
+    ((1, 3), (3, 0)),
+    ((0, 2), (1, 1)),
     ((1, 2), (2, 0)),
 )
 
@@ -251,15 +251,28 @@
     return step, zh * column + here, zh * column + there, (1 - zh) * column + there
 
 
-def prep_body(occupation_ref, plan_ref, notes_ref):
-    step, *owners = whereabouts()
+def masks_body(masks_ref):
+    step = whereabouts()[0]
+    lane = lax.broadcasted_iota(jnp.int32, (1, masks_ref.shape[1]), 1)
+    masks_ref[0:1] = jnp.where(lane == step, 1.0, 0.0)
+    masks_ref[1:2] = jnp.where(lane == SIZES[1] * SIZES[2] + step, 1.0, 0.0)
+
+
+def prep_body(occupation_ref, masks_ref, notes_ref):
+    _, *owners = whereabouts()
     lane = lax.broadcasted_iota(jnp.int32, (1, notes_ref.shape[1]), 1)
-    group = lax.axis_index("zl") * SIZES[4] + lax.axis_index("core")
     rows = [jnp.full(lane.shape, occupation_ref[owner * 2 + at]) for owner in owners for at in range(2)]
-    levels = [step, SIZES[1] * SIZES[2] + step, plan_ref[group * 2], plan_ref[group * 2 + 1]]
-    rows += [jnp.where(lane == level, 1.0, 0.0) for level in levels]
     for at, row in enumerate(rows):
         notes_ref[at : at + 1] = row
+    notes_ref[len(rows) : len(rows) + 2] = masks_ref[...]
+
+
+def picks_body(plan_ref, picks_ref):
+    slots = picks_ref.shape[0]
+    lane = lax.broadcasted_iota(jnp.int32, (1, picks_ref.shape[1]), 1)
+    group = lax.axis_index("zl") * SIZES[4] + lax.axis_index("core")
+    for slot in range(slots):
+        picks_ref[slot : slot + 1] = jnp.where(lane == plan_ref[group * slots + slot], 1.0, 0.0)
 
 
 def weights_of(notes_ref, which, own):
@@ -316,7 +329,7 @@
     out_ref[:, :, cells:] = jnp.broadcast_to(rows[None, :each], (chips, each, width - cells))
 
 
-def last_body(scale, notes_ref, pieces_ref, exchange_ref, slot_ref):
+def last_body(scale, picks_ref, pieces_ref, exchange_ref, slot_ref):
     chips, _, _ = pieces_ref.shape
     own, planes, cells = exchange_ref.shape
     total = pieces_ref[0]
@@ -326,7 +339,7 @@
         exchange_ref[a] = total[a * planes : (a + 1) * planes, :cells]
     levels = total[:1, cells:]
     for slot in range(slot_ref.shape[0]):
-        slot_ref[slot] = jnp.sum(levels * notes_ref[8 + slot : 9 + slot]) * scale
+        slot_ref[slot] = jnp.sum(levels * picks_ref[slot : slot + 1]) * scale
 
 
 def in_vmem(count):
@@ -373,7 +386,8 @@
             compiler_params=PARAMS,
         )(*arrays)
 
-    notes = call(prep_body, floats(16, 128), occupations, plan, smem=2, flops=1 << 30)
+    masks = call(masks_body, floats(2, 128), flops=1 << 30)
+    notes = call(prep_body, floats(8, 128), occupations, masks, smem=1)
     spectral = (floats(pairs * points, cells), floats(1, 128))
     work = 6 * pairs * points * cells * (pairs * points + 384)
     near_shaped, near_energy = call(
@@ -387,12 +401,13 @@
     everyone = lax.all_to_all(energies, ("y", "x", "core"), 0, 0, tiled=True)
     half = floats(rows // 2, cells)
     keep, send = call(back_body, (half, half), near, far, table, notes, near_shaped, far_shaped, flops=2 * work)
+    picks = call(picks_body, floats(slots, 128), plan, smem=1)
     received = lax.ppermute(send, AXES, routes(other_core))
     joined = call(join_body, floats(chips, each, cells + 128), keep, received, everyone)
     pieces = lax.all_to_all(joined, "zl", 0, 0, tiled=True)
     scale = -1.0 / (2.0 * total_orbitals * points**3)
     outs = (floats(own, each // own, cells), floats(slots))
-    return call(functools.partial(last_body, scale), outs, notes, pieces, smem_out=1)
+    return call(functools.partial(last_body, scale), outs, picks, pieces, smem_out=1)
 
 
 def solution(mesh):

time: 74.5 us -> 75.3 us (1.011)
  blocking collectives: 29 us -> 10.3 us
  waiting for transfers between devices: 8.56 us -> 21.1 us
  starting transfers between devices: 29.7 us -> 36.7 us
  local copies, waits for them, and re-layouts: 1.32 us -> 0.03 us
  Pallas kernels: 4.89 us -> 6.09 us
    all_to_all x1 -> x0, blocking collectives: 18.6 us -> none  [on_device(): pieces = lax.all_to_all(joined, 'zl', 0, 0, tiled=True)]
    all_to_all x0 -> x1, waiting for transfers between devices: none -> 11.2 us  [on_device(): pieces = lax.all_to_all(joined, 'zl', 0, 0, tiled=True)]
    all_to_all x0 -> x1, starting transfers between devices: none -> 6.98 us  [on_device(): pieces = lax.all_to_all(joined, 'zl', 0, 0, tiled=True)]
    ppermute x1, waiting for transfers between devices: 7.02 us -> 8.32 us  [on_device(): far = lax.ppermute(orbitals, AXES, routes(other_half))]
    unnamed x10, local copies, waits for them, and re-layouts: 1.32 us -> 0.03 us
    pallas_call x7 -> x9, Pallas kernels: 4.89 us -> 6.09 us  [call(): pl.pallas_call(body, out_shape=out_shape, in_specs=in_smem(smem) + in_vme...]
  transfers between devices with their start and end apart: 4 -> 5, of which waited for: 2 -> 3; matrix products, arithmetic and copies ran while one was open for 0% -> 0% of each run, Pallas kernels for 2% -> 3%
where the time goes in v7:
time: 75.3 us; the launch traced here: 75 us
  starting transfers between devices  36.7 us (49%)
  waiting for transfers between devices  21.1 us (28%)
  blocking collectives  10.3 us (14%)
  Pallas kernels  6.09 us (8%)
  between operations  0.79 us (1%)
    all_to_all x1, waiting for transfers between devices, on_device(): pieces = lax.all_to_all(joined, 'zl', 0, 0, tiled=True)  11.2 us
    ppermute x1, starting transfers between devices, on_device(): far = lax.ppermute(orbitals, AXES, routes(other_half))  11.1 us
    all_to_all x1, blocking collectives, on_device(): everyone = lax.all_to_all(energies, ('y', 'x', 'core'), 0, 0, tiled=True)  10.3 us
    ppermute x1, starting transfers between devices, on_device(): across = lax.ppermute(near_energy, AXES, routes(mirror))  9.29 us
    ppermute x1, waiting for transfers between devices, on_device(): far = lax.ppermute(orbitals, AXES, routes(other_half))  8.32 us
    ppermute x1, starting transfers between devices, on_device(): near = lax.ppermute(orbitals, AXES, routes(same_half))  7.43 us
    all_to_all x1, starting transfers between devices, on_device(): pieces = lax.all_to_all(joined, 'zl', 0, 0, tiled=True)  6.98 us
    pallas_call x9, Pallas kernels, call(): pl.pallas_call(body, out_shape=out_shape, in_specs=in_smem(smem) + in_vme...  6.09 us
  transfers between devices with their start and end apart: 5, of which 3 were waited for; matrix products, arithmetic and copies ran while one was open for 0% of the time, Pallas kernels for 3%

profile of v7, /device:TPU:32, one launch (start us, length us, event | category | flops | bytes accessed | tf_op | source)
XLA Modules:
  0.0 75.0 jit_solution(8459412440253122516)
XLA Ops:
  0.6 0.0 copy-start
  0.6 0.0 copy-start.1
  0.7 0.0 copy-start.3
  0.7 0.0 copy-start.2
  0.7 7.4 %collective-permute-start = (bf16[2,32,1024]{2,1,0:T(8,128)(2,1)}, bf16[2,32,1024]{2,1,0:T(8,128)(2,1)S(1)}, u32[]{:S(2)}, u32[]{:S(2)}) collective-permute-start(bf16[2,32,1024]{2,1,0:T(8,128)(2,1)} %mine_ref.3), channel_id=1, source_target_pairs={{0,160},{1,145},{2,178},{3,227},{4,244},{5,213},{6,6},{7,71},{8,24... | collective-permute-start | bytes 393224 | tf_op jit(solution)/shard_map/ppermute | solution.py:369
  8.1 11.1 %collective-permute-start.1 = (bf16[2,32,1024]{2,1,0:T(8,128)(2,1)}, bf16[2,32,1024]{2,1,0:T(8,128)(2,1)S(1)}, u32[]{:S(2)}, u32[]{:S(2)}) collective-permute-start(bf16[2,32,1024]{2,1,0:T(8,128)(2,1)} %mine_ref.3), channel_id=1, source_target_pairs={{0,430},{1,415},{2,444},{3,493},{4,506},{5,475},{6,264},{7,329},{8... | collective-permute-start | bytes 393224 | tf_op jit(solution)/shard_map/ppermute | solution.py:370
  19.2 0.0 copy-done.3
  19.2 0.6 shard_map.70.notes_ref
  19.8 0.0 collective-permute-done.partner_ref.near_ref
  19.9 1.0 %shard_map.71 = (f32[128,1024]{1,0:T(8,128)S(1)}, f32[1,128]{1,0:T(1,128)S(1)}) custom-call(bf16[2,32,1024]{2,1,0:T(8,128)(2,1)S(1)} %collective-permute-done.partner_ref.near_ref, bf16[2,32,1024]{2,1,0:T(8,128)(2,1)S(1)} %copy-done.1, bf16[3456,256]{1,0:T(8,128)(2,1)S(1)} %copy-done, f32[32,1024]{1,0:T(8,128)S(1)} %copy-done.2, ...), custom_call_target="tpu_custom_call" | custom-call | flops 402653184 | bytes 1048576 | tf_op jit(solution)/shard_map/pallas_call | solution.py:380
  20.9 8.3 %collective-permute-done.1.partner_ref.far_ref = bf16[2,32,1024]{2,1,0:T(8,128)(2,1)S(1)} collective-permute-done((bf16[2,32,1024]{2,1,0:T(8,128)(2,1)}, bf16[2,32,1024]{2,1,0:T(8,128)(2,1)S(1)}, u32[]{:S(2)}, u32[]{:S(2)}) %collective-permute-start.1) | collective-permute-done | bytes 131104 | tf_op jit(solution)/shard_map/ppermute | solution.py:370
  29.2 1.0 %shard_map.72 = (f32[128,1024]{1,0:T(8,128)S(1)}, f32[1,128]{1,0:T(1,128)S(1)}) custom-call(bf16[2,32,1024]{2,1,0:T(8,128)(2,1)S(1)} %collective-permute-done.1.partner_ref.far_ref, bf16[2,32,1024]{2,1,0:T(8,128)(2,1)S(1)} %copy-done.1, bf16[3456,256]{1,0:T(8,128)(2,1)S(1)} %copy-done, f32[32,1024]{1,0:T(8,128)S(1)} %copy-done.2, ...), custom_call_target="tpu_custom_call" | custom-call | flops 402653184 | bytes 1048576 | tf_op jit(solution)/shard_map/pallas_call | solution.py:380
  30.3 0.0 copy-start.4
  30.3 1.5 %shard_map.73 = (f32[32,1024]{1,0:T(8,128)S(1)}, f32[32,1024]{1,0:T(8,128)S(1)}) custom-call(bf16[2,32,1024]{2,1,0:T(8,128)(2,1)S(1)} %collective-permute-done.partner_ref.near_ref, bf16[2,32,1024]{2,1,0:T(8,128)(2,1)S(1)} %collective-permute-done.1.partner_ref.far_ref, bf16[3456,256]{1,0:T(8,128)(2,1)S(1)} %copy-done, f32[8,128]{1,0:T(8,128)S(1)} %shard_map.70.notes_ref, ...), custom_call_target="tpu_custom_call" | custom-call | flops 805306368 | bytes 1048576 | tf_op jit(solution)/shard_map/pallas_call | solution.py:380
  31.8 1.9 %collective-permute-start.2 = (f32[32,1024]{1,0:T(8,128)S(1)}, f32[32,1024]{1,0:T(8,128)S(1)}, u32[]{:S(2)}, u32[]{:S(2)}) collective-permute-start(f32[32,1024]{1,0:T(8,128)S(1)} %get-tuple-element.11), channel_id=1, source_target_pairs={{0,1},{1,0},{2,3},{3,2},{4,5},{5,4},{6,7},{7,6},{8,9},{9,8},{10,11... | collective-permute-start | bytes 393224 | tf_op jit(solution)/shard_map/ppermute | solution.py:405
  33.7 9.3 %collective-permute-start.3 = (f32[1,128]{1,0:T(1,128)S(1)}, f32[1,128]{1,0:T(1,128)S(1)}, u32[]{:S(2)}, u32[]{:S(2)}) collective-permute-start(f32[1,128]{1,0:T(1,128)S(1)} %get-tuple-element.12.near_ref), channel_id=1, source_target_pairs={{0,270},{1,271},{2,268},{3,269},{4,266},{5,267},{6,264},{7,265},{8... | collective-permute-start | bytes 1544 | tf_op jit(solution)/shard_map/ppermute | solution.py:396
  43.0 1.5 %collective-permute-done.3.across_ref = f32[1,128]{1,0:T(1,128)S(1)} collective-permute-done((f32[1,128]{1,0:T(1,128)S(1)}, f32[1,128]{1,0:T(1,128)S(1)}, u32[]{:S(2)}, u32[]{:S(2)}) %collective-permute-start.3) | collective-permute-done | bytes 544 | tf_op jit(solution)/shard_map/ppermute | solution.py:396
  44.6 10.3 %all_to_all.10.energies_ref = f32[32,1,128]{2,1,0:T(1,128)S(1)} all-to-all(f32[32,1,128]{2,1,0:T(1,128)S(1)} %shard_map.74), channel_id=1, replica_groups=mesh['zh'=2,'y'=4,'x'=4,'zl'=8,'core'=2] {'y','x','core'}, dimensions={0} | all-to-all | bytes 32768 | tf_op jit(solution)/shard_map/all_to_all | solution.py:401
  54.9 0.0 collective-permute-done.2.received_ref
  54.9 0.7 shard_map.75
  55.6 7.0 %all-to-all-start.1 = ((f32[8,4,1152]{2,1,0:T(4,128)}), f32[8,4,1152]{2,1,0:T(4,128)S(1)}, u32[]{:S(2)}, u32[]{:S(2)}) async-start(f32[8,4,1152]{2,1,0:T(4,128)} %shard_map.75), calls=%async_computation.1 | async-start | bytes 294912 | tf_op jit(solution)/shard_map/all_to_all | solution.py:407
  62.6 0.6 shard_map.68.picks_ref
  63.2 11.2 %all-to-all-done.1.pieces_ref = f32[8,4,1152]{2,1,0:T(4,128)S(1)} async-done(((f32[8,4,1152]{2,1,0:T(4,128)}), f32[8,4,1152]{2,1,0:T(4,128)S(1)}, u32[]{:S(2)}, u32[]{:S(2)}) %all-to-all-start.1) | async-done | bytes 147488 | tf_op jit(solution)/shard_map/all_to_all | solution.py:407
  74.4 0.6 shard_map.76
  (6 shorter events, 0.0 us)
Async XLA Ops:
  0.6 19.2 %copy-start = (bf16[3456,256]{1,0:T(8,128)(2,1)S(1)}, bf16[3456,256]{1,0:T(8,128)(2,1)}, u32[]{:S(2)}) copy-start(bf16[3456,256]{1,0:T(8,128)(2,1)} %constant.2.clone.table_ref) | copy-start | bytes 5308420
  0.6 19.2 %copy-start.1 = (bf16[2,32,1024]{2,1,0:T(8,128)(2,1)S(1)}, bf16[2,32,1024]{2,1,0:T(8,128)(2,1)}, u32[]{:S(2)}) copy-start(bf16[2,32,1024]{2,1,0:T(8,128)(2,1)} %mine_ref.3) | copy-start | bytes 393220
  0.7 18.6 %copy-start.3 = (f32[64]{0:T(128)S(1)}, f32[64]{0:T(128)}, u32[]{:S(2)}) copy-start(f32[64]{0:T(128)} %occupation_ref.1) | copy-start | bytes 772
  0.7 19.2 %copy-start.2 = (f32[32,1024]{1,0:T(8,128)S(1)}, f32[32,1024]{1,0:T(8,128)}, u32[]{:S(2)}) copy-start(f32[32,1024]{1,0:T(8,128)} %kernel_ref.3) | copy-start | bytes 393220
  0.7 19.2 %collective-permute-start = (bf16[2,32,1024]{2,1,0:T(8,128)(2,1)}, bf16[2,32,1024]{2,1,0:T(8,128)(2,1)S(1)}, u32[]{:S(2)}, u32[]{:S(2)}) collective-permute-start(bf16[2,32,1024]{2,1,0:T(8,128)(2,1)} %mine_ref.3), channel_id=1, source_target_pairs={{0,160},{1,145},{2,178},{3,227},{4,244},{5,213},{6,6},{7,71},{8,24... | collective-permute-start | bytes 393224 | tf_op jit(solution)/shard_map/ppermute | solution.py:369
  8.1 21.1 %collective-permute-start.1 = (bf16[2,32,1024]{2,1,0:T(8,128)(2,1)}, bf16[2,32,1024]{2,1,0:T(8,128)(2,1)S(1)}, u32[]{:S(2)}, u32[]{:S(2)}) collective-permute-start(bf16[2,32,1024]{2,1,0:T(8,128)(2,1)} %mine_ref.3), channel_id=1, source_target_pairs={{0,430},{1,415},{2,444},{3,493},{4,506},{5,475},{6,264},{7,329},{8... | collective-permute-start | bytes 393224 | tf_op jit(solution)/shard_map/ppermute | solution.py:370
  30.3 32.3 %copy-start.4 = (s32[32]{0:T(128)S(1)}, s32[32]{0:T(128)}, u32[]{:S(2)}) copy-start(s32[32]{0:T(128)} %plan_ref.1) | copy-start | bytes 388
  31.8 23.1 %collective-permute-start.2 = (f32[32,1024]{1,0:T(8,128)S(1)}, f32[32,1024]{1,0:T(8,128)S(1)}, u32[]{:S(2)}, u32[]{:S(2)}) collective-permute-start(f32[32,1024]{1,0:T(8,128)S(1)} %get-tuple-element.11), channel_id=1, source_target_pairs={{0,1},{1,0},{2,3},{3,2},{4,5},{5,4},{6,7},{7,6},{8,9},{9,8},{10,11... | collective-permute-start | bytes 393224 | tf_op jit(solution)/shard_map/ppermute | solution.py:405
  33.7 10.8 %collective-permute-start.3 = (f32[1,128]{1,0:T(1,128)S(1)}, f32[1,128]{1,0:T(1,128)S(1)}, u32[]{:S(2)}, u32[]{:S(2)}) collective-permute-start(f32[1,128]{1,0:T(1,128)S(1)} %get-tuple-element.12.near_ref), channel_id=1, source_target_pairs={{0,270},{1,271},{2,268},{3,269},{4,266},{5,267},{6,264},{7,265},{8... | collective-permute-start | bytes 1544 | tf_op jit(solution)/shard_map/ppermute | solution.py:396
  55.6 18.7 %all-to-all-start.1 = ((f32[8,4,1152]{2,1,0:T(4,128)}), f32[8,4,1152]{2,1,0:T(4,128)S(1)}, u32[]{:S(2)}, u32[]{:S(2)}) async-start(f32[8,4,1152]{2,1,0:T(4,128)} %shard_map.75), calls=%async_computation.1 | async-start | bytes 294912 | tf_op jit(solution)/shard_map/all_to_all | solution.py:407
